TPU v7x, 128 devices: a whole 4x4x4 slice. The times are simulated.
128 devices in a mesh: seq: 32 (over x_hi, y, z), head: 4 (over x_lo, core).
Axes of the slice: x: 4 (x_hi: 2, x_lo: 2; x = x_hi * 2 + x_lo), y: 4, z: 4, core: 2. Of those that a mesh axis runs over, the one named last changes fastest.
Arguments:
- queries: bfloat16 [16384, 5120], P(('seq', 'head')), may hold values from -163 to 163
- keys: bfloat16 [16384, 5120], P(('seq', 'head')), may hold values from -6.5 to 6.5
- values: bfloat16 [16384, 5120], P(('seq', 'head')), may hold values from -6 to 6
- step_rate: bfloat16 [16384, 8], P(('seq', 'head')), may hold values from 0.099609375 to 1
- doc_start: int32 [16384], P('seq'), may hold values from 0 to 16383, as said below
- window_len: int32 [40], replicated, may hold values from 512 to 2048, as said below
- head_order: int32 [40], replicated, may hold values from 0 to 39, each once
- learn_rate: float32 [8], replicated, may hold values from 0.01 to 0.04
- w_gate: bfloat16 [8, 640, 640], P('head'), may hold values from -0.25 to 0.25
- w_up: bfloat16 [8, 640, 640], P('head'), may hold values from -0.25 to 0.25
- w_down: bfloat16 [8, 640, 640], P('head'), may hold values from -0.25 to 0.25
Outputs:
- mixed: bfloat16 [16384, 5120], P(('seq', 'head'))
Inputs may be any that keep to these rules, and one draw needn't show every extreme that they name: doc_start[t] is the first position of the document holding t: at most t, never falling, equal to t where a document begins; a document begins at position 16383. `window_len`: some head has a window of exactly 2048. `head_order`: a permutation of the 40 heads.
All inputs are finite; a program needn't handle non-finite values.
Results may differ from a plain program's by a relative error of at most 0.03.
Values may be sent and summed in bfloat16 or wider, within the bound.
A program may use at most 128 MiB of HBM per device.

v0:
```python
import jax
import jax.numpy as jnp
from jax import lax
from jax.sharding import PartitionSpec as P

WINDOW = 2048


def passed_along(x, axis, by):
    count = lax.axis_size(axis)
    pairs = [(i, i + by) for i in range(count) if 0 <= i + by < count]
    return lax.ppermute(x, axis, pairs)


def attend(query_block, key_block, value_block, start_row, window_size, doc_first):
    block_rows = query_block.shape[0]
    key_rows = key_block.shape[0]
    score_scale = query_block.shape[1] ** (-0.5)
    scores = (
        jnp.einsum("qd,kd->qk", query_block, key_block, preferred_element_type=jnp.float32)
        * score_scale
    )
    query_pos = start_row + jnp.arange(block_rows, dtype=jnp.int32)
    key_pos = start_row - (key_rows - block_rows) + jnp.arange(key_rows, dtype=jnp.int32)
    valid = (
        (key_pos[None, :] <= query_pos[:, None])
        & (key_pos[None, :] > query_pos[:, None] - window_size)
        & (key_pos[None, :] >= doc_first[:, None])
    )
    scores = jnp.where(valid, scores, -1e30)
    row_max = jnp.max(scores, axis=1, keepdims=True)
    weights = jnp.where(valid, jnp.exp(scores - row_max), 0.0)
    weights_bf = (weights / jnp.sum(weights, axis=1, keepdims=True)).astype(jnp.bfloat16)
    return jnp.dot(weights_bf, value_block, preferred_element_type=jnp.float32)


def refresh(old, grad, factor):
    moved = old.astype(jnp.float32) - factor[:, None, None] * grad
    kept_norm = jnp.sqrt(jnp.sum(old.astype(jnp.float32) ** 2, axis=1, keepdims=True))
    new_norm = jnp.sqrt(jnp.sum(moved * moved, axis=1, keepdims=True) + 1e-06)
    return (moved * (kept_norm / new_norm)).astype(jnp.bfloat16)


def per_device(
    queries,
    keys,
    values,
    step_rate,
    doc_start,
    window_len,
    head_order,
    learn_rate,
    w_gate,
    w_up,
    w_down,
):
    head_count = head_order.shape[0]
    width_full = queries.shape[1]
    head_size = width_full // head_count
    token_rows = queries.shape[0]

    def reorder(x):
        return x.reshape(token_rows, head_count, head_size)[:, head_order].reshape(
            token_rows, width_full
        )

    q_local, k_local, v_local, rate_local = (
        lax.all_to_all(reorder(queries), "head", split_axis=1, concat_axis=0, tiled=True),
        lax.all_to_all(reorder(keys), "head", split_axis=1, concat_axis=0, tiled=True),
        lax.all_to_all(reorder(values), "head", split_axis=1, concat_axis=0, tiled=True),
        lax.all_to_all(step_rate, "head", split_axis=1, concat_axis=0, tiled=True),
    )
    group_rows = q_local.shape[0]
    group_width = q_local.shape[1]
    local_heads = group_width // head_size
    paired = jnp.stack([k_local, v_local])
    needed = (WINDOW + group_rows - 1) // group_rows
    earlier = []
    carried = paired
    for number in range(needed):
        carried = passed_along(carried, "seq", 1)
        earlier = [carried] + earlier
    buffer = jnp.concatenate(earlier + [paired], axis=1)
    block_rows = min(512, group_rows)
    block_count = group_rows // block_rows
    offset = lax.axis_index("seq") * group_rows
    chosen = lax.dynamic_slice_in_dim(head_order, lax.axis_index("head") * local_heads, local_heads)
    windows = jnp.take(window_len, chosen)
    query_heads = q_local.reshape(group_rows, local_heads, head_size).transpose(1, 0, 2)
    key_heads = buffer[0].reshape(WINDOW + group_rows, local_heads, head_size).transpose(1, 0, 2)
    value_heads = buffer[1].reshape(WINDOW + group_rows, local_heads, head_size).transpose(1, 0, 2)

    def one_head(packed):
        query_one, key_one, value_one, window_size = packed

        def one_block(block_index):
            start_row = block_index * block_rows
            return attend(query_one, key_one, value_one, offset + start_row, window_size, doc_start)

        return lax.map(one_block, jnp.arange(block_count, dtype=jnp.int32)).reshape(
            group_rows, head_size
        )

    attended = (
        lax.map(one_head, (query_heads, key_heads, value_heads, windows))
        .transpose(1, 0, 2)
        .reshape(group_rows, group_width)
    )
    fast_local = w_gate.shape[0]
    fast_width = group_width // fast_local

    def normed(x):
        as_float = x.astype(jnp.float32).reshape(group_rows, fast_local, fast_width)
        return (
            as_float * lax.rsqrt(jnp.mean(as_float * as_float, axis=-1, keepdims=True) + 1e-06)
        ).astype(jnp.bfloat16)

    k_norm = normed(k_local)
    q_norm = normed(q_local)
    v_fast = v_local.reshape(group_rows, fast_local, fast_width)
    pre_gate = jnp.einsum("tfi,fih->tfh", k_norm, w_gate, preferred_element_type=jnp.float32)
    pre_up = jnp.einsum("tfi,fih->tfh", k_norm, w_up, preferred_element_type=jnp.float32)
    sigmoid_gate = jax.nn.sigmoid(pre_gate)
    lifted = pre_gate * sigmoid_gate
    hidden = (lifted * pre_up).astype(jnp.bfloat16)
    target = (rate_local.astype(jnp.float32)[:, :, None] * v_fast.astype(jnp.float32)).astype(
        jnp.bfloat16
    )
    back_hidden = -jnp.einsum("tfo,fho->tfh", target, w_down, preferred_element_type=jnp.float32)
    grad_down = -jnp.einsum("tfh,tfo->fho", hidden, target, preferred_element_type=jnp.float32)
    back_gate = (
        back_hidden * pre_up * sigmoid_gate * (1.0 + pre_gate * (1.0 - sigmoid_gate))
    ).astype(jnp.bfloat16)
    back_up = (back_hidden * lifted).astype(jnp.bfloat16)
    grad_gate = jnp.einsum("tfi,tfh->fih", k_norm, back_gate, preferred_element_type=jnp.float32)
    grad_up = jnp.einsum("tfi,tfh->fih", k_norm, back_up, preferred_element_type=jnp.float32)
    head_rates = lax.dynamic_slice_in_dim(
        learn_rate, lax.axis_index("head") * fast_local, fast_local
    )
    old_weights = (w_gate, w_up, w_down)
    summed = (
        lax.psum(grad_gate.astype(jnp.bfloat16), "seq").astype(jnp.float32),
        lax.psum(grad_up.astype(jnp.bfloat16), "seq").astype(jnp.float32),
        lax.psum(grad_down.astype(jnp.bfloat16), "seq").astype(jnp.float32),
    )
    refreshed = [
        refresh(
            old_weights[number],
            summed[number],
            head_rates * lax.rsqrt(jnp.mean(summed[number] * summed[number], axis=(1, 2)) + 1e-06),
        )
        for number in range(3)
    ]
    new_gate, new_up, new_down = (refreshed[0], refreshed[1], refreshed[2])
    gate_q = jnp.einsum("tfi,fih->tfh", q_norm, new_gate, preferred_element_type=jnp.float32)
    up_q = jnp.einsum("tfi,fih->tfh", q_norm, new_up, preferred_element_type=jnp.float32)
    applied = (jax.nn.silu(gate_q) * up_q).astype(jnp.bfloat16)
    produced = jnp.einsum(
        "tfh,fho->tfo", applied, new_down, preferred_element_type=jnp.float32
    ).reshape(group_rows, group_width)
    summed_out = (attended + produced).astype(jnp.bfloat16)
    regrouped = lax.all_to_all(summed_out, "head", split_axis=0, concat_axis=1, tiled=True)
    inverse = (
        jnp.zeros((head_count,), jnp.int32)
        .at[head_order]
        .set(jnp.arange(head_count, dtype=jnp.int32))
    )
    return regrouped.reshape(token_rows, head_count, head_size)[:, inverse].reshape(
        token_rows, width_full
    )


def solution(mesh):
    placed = (
        P(("seq", "head"), None),
        P(("seq", "head"), None),
        P(("seq", "head"), None),
        P(("seq", "head"), None),
        P("seq"),
        P(),
        P(),
        P(),
        P("head", None, None),
        P("head", None, None),
        P("head", None, None),
    )
    return jax.shard_map(
        per_device, mesh=mesh, in_specs=placed, out_specs=P(("seq", "head"), None), check_vma=False
    )
```

profile of v0, /device:TPU:4, one launch (start us, length us, event | category | flops | bytes accessed | tf_op | source)
XLA Modules:
  0.0 697.8 jit_solution(16437262330995873113)
XLA Ops:
  27.3 9.7 %all-to-all-done.1 = bf16[128,4,1280]{0,2,1:T(8,128)(2,1)S(1)} async-done(((bf16[128,4,1280]{0,2,1:T(8,128)(2,1)}), bf16[128,4,1280]{0,2,1:T(8,128)(2,1)S(1)}, u32[]{:S(2)}, u32[]{:S(2)}) %all-to-all-start.1) | async-done | bytes 1310752 | tf_op jit(solution)/shard_map/all_to_all | solution.py:69
  37.0 4.3 all-to-all-start.2
  52.1 6.6 all-to-all-done.2
  62.2 4.4 reshape.156
  71.3 4.2 collective-permute-start
  88.1 64.2 %collective-permute-done = bf16[2,512,1280]{2,1,0:T(8,128)(2,1)} collective-permute-done((bf16[2,512,1280]{2,1,0:T(8,128)(2,1)}, bf16[2,512,1280]{2,1,0:T(8,128)(2,1)}, u32[]{:S(2)}, u32[]{:S(2)}) %collective-permute-start) | collective-permute-done | bytes 2621472 | tf_op jit(solution)/shard_map/ppermute | solution.py:12
  161.6 81.0 %collective-permute-done.1 = bf16[2,512,1280]{2,1,0:T(8,128)(2,1)} collective-permute-done((bf16[2,512,1280]{2,1,0:T(8,128)(2,1)}, bf16[2,512,1280]{2,1,0:T(8,128)(2,1)}, u32[]{:S(2)}, u32[]{:S(2)}) %collective-permute-start.1) | collective-permute-done | bytes 2621472 | tf_op jit(solution)/shard_map/ppermute | solution.py:12
  255.0 7.4 %copy.196 = bf16[4,128,1280]{1,0,2:T(4,128)(2,1)} copy(bf16[4,128,1280]{1,2,0:T(8,128)(2,1)} %bitcast.151) | data formatting | bytes 2621440 | tf_op jit(solution)/shard_map/all_to_all | solution.py:68
  265.9 200.8 %all-reduce.3.cloned.1.call-done = (bf16[2,640,640]{2,1,0:T(8,128)(2,1)}, bf16[2,640,640]{2,1,0:T(8,128)(2,1)}, bf16[2,640,640]{2,1,0:T(8,128)(2,1)}) async-done(((bf16[2,640,640]{2,1,0:T(8,128)(2,1)}, bf16[2,640,640]{2,1,0:T(8,128)(2,1)}, bf16[2,640,640]{2,1,0:T(8,128)(2,1)}), (bf16[2,640,640]{2,1,0:T(8,128)(2,1)}, bf16[2,640,640]{2,1,0:T(8,128)(2,1)}, ...) | async-done | bytes 4915216 | tf_op jit(solution)/shard_map/psum | solution.py:144
  481.1 8.3 %convolution_bitcast_fusion = f32[512,2,640]{0,2,1:T(8,128)} fusion(bf16[2,640,640]{2,1,0:T(8,128)(2,1)} %get-tuple-element.234, bf16[2,640,640]{2,1,0:T(8,128)(2,1)} %param.23, f32[2,640]{1,0:T(2,128)S(1)} %rsqrt_multiply_fusion.2, f32[2]{0:T(128)S(1)} %get-tuple-element.245, f32[2,640,512]{1,2,0:T(8,128)} %fusion.35, ...), kind=kOutput, calls=%fused_computation.83 | convolution fusion | flops 1692794880 | bytes 14432272 | tf_op jit(solution)/shard_map/tfh,fho->tfo/dot_general | solution.py:158
  492.5 26.9 %collective-permute-done.3 = bf16[2,512,1280]{2,1,0:T(8,128)(2,1)} collective-permute-done((bf16[2,512,1280]{2,1,0:T(8,128)(2,1)}, bf16[2,512,1280]{2,1,0:T(8,128)(2,1)}, u32[]{:S(2)}, u32[]{:S(2)}) %collective-permute-start.3) | collective-permute-done | bytes 2621472 | tf_op jit(solution)/shard_map/ppermute | solution.py:12
  527.8 5.0 fusion.58
  532.8 9.6 %copy.205 = bf16[1,2560,1280]{1,2,0:T(8,128)(2,1)} copy(bf16[1,2560,1280]{2,1,0:T(8,128)(2,1)} %get-tuple-element.242) | data formatting | bytes 13107200 | tf_op jit(solution)/shard_map/slice | solution.py:90
  542.3 9.6 %copy.206 = bf16[1,2560,1280]{1,2,0:T(8,128)(2,1)} copy(bf16[1,2560,1280]{2,1,0:T(8,128)(2,1)} %get-tuple-element.241) | data formatting | bytes 13107200 | tf_op jit(solution)/shard_map/slice | solution.py:91
  551.9 102.9 %while.17 = (s32[]{:T(128)}, f32[10,512,128]{2,1,0:T(8,128)}, s32[]{:T(128)}, s32[]{:T(128)}, s32[10]{0:T(128)S(1)}, /*index=5*/s32[512]{0:T(512)S(1)}, bf16[10,...) while((s32[]{:T(128)}, f32[10,512,128]{2,1,0:T(8,128)}, ...), condition=%wide.region_3.4_spmd, body=%wide.region_0.3_spmd.sunk | while | flops 703859200 | bytes 17508476 | solution.py:105
  558.4 3.8 fusion.75
  578.9 3.8 fusion.75
  589.2 3.8 fusion.75
  599.5 3.8 fusion.75
  620.1 3.8 fusion.75
  630.4 3.8 fusion.75
  640.7 3.8 fusion.75
  658.0 4.0 reshape.150
  670.3 16.3 %all-to-all-done.4 = bf16[4,128,1280]{1,2,0:T(8,128)(2,1)S(1)} async-done(((bf16[4,128,1280]{1,2,0:T(8,128)(2,1)}), bf16[4,128,1280]{1,2,0:T(8,128)(2,1)S(1)}, u32[]{:S(2)}, u32[]{:S(2)}) %all-to-all-start.4) | async-done | bytes 1310752 | tf_op jit(solution)/shard_map/all_to_all | solution.py:162
  (189 shorter events, 194.2 us)
Async XLA Ops:
  6.5 238.2 %copy-start = (s32[40]{0:T(128)S(1)}, s32[40]{0:T(128)}, u32[]{:S(2)}) copy-start(s32[40]{0:T(128)} %param.18) | copy-start | bytes 484
  6.5 9.6 %all-to-all-start.3 = ((bf16[128,4,2]{0,2,1:T(2,128)(2,1)}), bf16[128,4,2]{0,2,1:T(2,128)(2,1)S(1)}, u32[]{:S(2)}, u32[]{:S(2)}) async-start(bf16[128,4,2]{0,2,1:T(2,128)(2,1)} %bitcast.165), calls=%async_computation.3 | async-start | bytes 4096 | tf_op jit(solution)/shard_map/all_to_all | solution.py:71
  16.1 20.9 %all-to-all-start.1 = ((bf16[128,4,1280]{0,2,1:T(8,128)(2,1)}), bf16[128,4,1280]{0,2,1:T(8,128)(2,1)S(1)}, u32[]{:S(2)}, u32[]{:S(2)}) async-start(bf16[128,4,1280]{0,2,1:T(8,128)(2,1)} %bitcast.12), calls=%async_computation.1 | async-start | bytes 2621440 | tf_op jit(solution)/shard_map/all_to_all | solution.py:69
  37.0 6.0 copy-start.10
  37.0 21.6 %all-to-all-start.2 = ((bf16[128,4,1280]{0,2,1:T(8,128)(2,1)}), bf16[128,4,1280]{0,2,1:T(8,128)(2,1)}, u32[]{:S(2)}, u32[]{:S(2)}) async-start(bf16[128,4,1280]{0,2,1:T(8,128)(2,1)} %bitcast.17), calls=%async_computation.2 | async-start | bytes 2621440 | tf_op jit(solution)/shard_map/all_to_all | solution.py:70
  41.3 425.4 %all-reduce.3.cloned.1.call-start = ((), (), s32[]{:S(2)}) async-start(), calls=%async_computation.5 | async-start | bytes 9830400 | tf_op jit(solution)/shard_map/psum | solution.py:144
  69.3 6.3 copy-start.2
  69.3 6.3 copy-start.12
  71.3 5.6 copy-start.13
  71.3 5.6 copy-start.16
  71.3 80.9 %collective-permute-start = (bf16[2,512,1280]{2,1,0:T(8,128)(2,1)}, bf16[2,512,1280]{2,1,0:T(8,128)(2,1)}, u32[]{:S(2)}, u32[]{:S(2)}) collective-permute-start(bf16[2,512,1280]{2,1,0:T(8,128)(2,1)} %pad_maximum_fusion), channel_id=1, source_target_pairs={{0,4},{4,8},{8,12},{12,16},{16,20},{20,24},{24,28},{28,32},{32,36}... | collective-permute-start | bytes 7864328 | tf_op jit(solution)/shard_map/ppermute | solution.py:12
  88.0 66.1 %copy-start.21 = (bf16[128,5120]{1,0:T(8,128)(2,1)S(1)}, bf16[128,5120]{1,0:T(8,128)(2,1)}, u32[]{:S(2)}) copy-start(bf16[128,5120]{1,0:T(8,128)(2,1)} %param.13) | copy-start | bytes 3932164
  152.2 90.3 %collective-permute-start.1 = (bf16[2,512,1280]{2,1,0:T(8,128)(2,1)}, bf16[2,512,1280]{2,1,0:T(8,128)(2,1)}, u32[]{:S(2)}, u32[]{:S(2)}) collective-permute-start(bf16[2,512,1280]{2,1,0:T(8,128)(2,1)} %collective-permute-done), channel_id=1, source_target_pairs={{0,4},{4,8},{8,12},{12,16},{16,20},{20,24},{24,28},{28,32},{32,36}... | collective-permute-start | bytes 7864328 | tf_op jit(solution)/shard_map/ppermute | solution.py:12
  156.6 88.8 %copy-start.24 = (s32[40]{0:T(128)S(1)}, s32[40]{0:T(128)}, u32[]{:S(2)}) copy-start(s32[40]{0:T(128)} %param.19) | copy-start | bytes 484
  158.0 87.5 %all-to-all-start = ((bf16[128,4,1280]{0,2,1:T(8,128)(2,1)}), bf16[128,4,1280]{0,2,1:T(8,128)(2,1)S(1)}, u32[]{:S(2)}, u32[]{:S(2)}) async-start(bf16[128,4,1280]{0,2,1:T(8,128)(2,1)} %bitcast.7), calls=%async_computation | async-start | bytes 2621440 | tf_op jit(solution)/shard_map/all_to_all | solution.py:68
  242.6 229.9 %collective-permute-start.2 = (bf16[2,512,1280]{2,1,0:T(8,128)(2,1)}, bf16[2,512,1280]{2,1,0:T(8,128)(2,1)}, u32[]{:S(2)}, u32[]{:S(2)}) collective-permute-start(bf16[2,512,1280]{2,1,0:T(8,128)(2,1)} %collective-permute-done.1), channel_id=1, source_target_pairs={{0,4},{4,8},{8,12},{12,16},{16,20},{20,24},{24,28},{28,32},{32,36}... | collective-permute-start | bytes 7864328 | tf_op jit(solution)/shard_map/ppermute | solution.py:12
  265.9 205.6 %copy-start.25 = (f32[8]{0:T(128)S(1)}, f32[8]{0:T(128)}, u32[]{:S(2)}) copy-start(f32[8]{0:T(128)} %param.20) | copy-start | bytes 100
  466.7 4.8 copy-start.19
  469.4 6.7 copy-start.3
  471.5 5.5 copy-start.17
  471.5 5.5 copy-start.18
  472.5 46.9 %collective-permute-start.3 = (bf16[2,512,1280]{2,1,0:T(8,128)(2,1)}, bf16[2,512,1280]{2,1,0:T(8,128)(2,1)}, u32[]{:S(2)}, u32[]{:S(2)}) collective-permute-start(bf16[2,512,1280]{2,1,0:T(8,128)(2,1)} %collective-permute-done.2), channel_id=1, source_target_pairs={{0,4},{4,8},{8,12},{12,16},{16,20},{20,24},{24,28},{28,32},{32,36}... | collective-permute-start | bytes 7864328 | tf_op jit(solution)/shard_map/ppermute | solution.py:12
  542.3 9.6 %copy-start.22 = (s32[512]{0:T(512)S(1)}, s32[512]{0:T(512)}, u32[]{:S(2)}) copy-start(s32[512]{0:T(512)} %param.17) | copy-start | bytes 6148
  665.9 20.8 %all-to-all-start.4 = ((bf16[4,128,1280]{1,2,0:T(8,128)(2,1)}), bf16[4,128,1280]{1,2,0:T(8,128)(2,1)S(1)}, u32[]{:S(2)}, u32[]{:S(2)}) async-start(bf16[4,128,1280]{1,2,0:T(8,128)(2,1)} %copy.227), calls=%async_computation.4 | async-start | bytes 2621440 | tf_op jit(solution)/shard_map/all_to_all | solution.py:162
  (12 other events, 35.6 us)
Sparse Core Ops, SparseCore 0:
  88.2 378.4 all-reduce.2
where the time goes:
time: 706 us; the launch traced here: 698 us
  waiting for transfers between devices  406 us (58%)
  local copies, waits for them, and re-layouts  104 us (15%)
  matrix products  92.5 us (13%)
  other arithmetic  50.5 us (7%)
  starting transfers between devices  30.4 us (4%)
  between operations  14.4 us (2%)
    psum x1, waiting for transfers between devices, per_device(): lax.psum(grad_down.astype(jnp.bfloat16), 'seq').astype(jnp.float32)  201 us
    ppermute x4, waiting for transfers between devices, passed_along(): return lax.ppermute(x, axis, pairs)  172 us
    dot_general x10, matrix products, attend(): return jnp.dot(weights_bf, value_block, preferred_element_type=jnp.float32)  38.3 us
    dot_general x10, matrix products, attend(): jnp.einsum('qd,kd->qk', query_block, key_block, preferred_element_type=jn...  30.3 us
    reduce_sum x10, other arithmetic, attend(): jnp.sum(weights, axis=1, keepdims=True)  22 us
    all_to_all x1, waiting for transfers between devices, per_device(): lax.all_to_all(summed_out, 'head', split_axis=0, concat_axis=1, tiled=True)  16.3 us
    slice x2, local copies, waits for them, and re-layouts, per_device(): buffer[1].reshape(WINDOW + group_rows, local_heads, head_size)  14.5 us
  transfers between devices with their start and end apart: 10, of which 7 were waited for; matrix products, arithmetic and copies ran while one was open for 12% of the time, Pallas kernels for 0%

commit v1 on v0

v1 whole, which is shorter than its diff:
```python
import functools

import jax
import jax.numpy as jnp
from jax import lax
from jax.experimental import pallas as pl
from jax.experimental.pallas import tpu as pltpu
from jax.sharding import PartitionSpec as P

MESH = pl.DeviceIdType.MESH
ANY = pl.BlockSpec(memory_space=pl.ANY)
VM = pl.BlockSpec(memory_space=pltpu.VMEM)
HD = 128
GH = 5
FW = 640
TB = 128
KVR = 272
ROWS = 8
F32 = jnp.float32
BF16 = jnp.bfloat16

SEND_ORDER = ((0, 1), (1, 0), (3, 0), (1, 1), (3, 1), (2, 0), (2, 1))
WAIT_ORDER = ((0, 0), (0, 1), (1, 0), (3, 0), (1, 1), (3, 1), (2, 0), (2, 1))


def coords():
    s, h = lax.axis_index("seq"), lax.axis_index("head")
    return lax.div(s, 4), lax.rem(s, 4), lax.div(h, 2), lax.rem(h, 2)


def dev(row, z, x, c):
    return (row * 4 + z, x * 2 + c)


def sem_wait_bytes(ref, sem):
    pltpu.make_async_copy(ref, ref, sem).wait()


def signal(sem, device):
    pl.semaphore_signal(sem, inc=1, device_id=device, device_id_type=MESH)


def rcopy(src, dst, ssem, rsem, device):
    return pltpu.make_async_remote_copy(
        src_ref=src, dst_ref=dst, send_sem=ssem, recv_sem=rsem, device_id=device, device_id_type=MESH
    )


def reorder_kernel(order, q, k, v, rate, kvr, qo):
    g = pl.program_id(0)
    for j in range(GH):
        at = pl.ds(pl.multiple_of(order[g * GH + j] * HD, HD), HD)
        to = slice(j * HD, (j + 1) * HD)
        kvr[0, 0:TB, to] = k[:, at]
        kvr[0, TB : 2 * TB, to] = v[:, at]
        qo[0, :, to] = q[:, at]
    kvr[0, 2 * TB :, 0:HD] = rate[0]
    kvr[0, 2 * TB :, HD:] = jnp.zeros((KVR - 2 * TB, FW - HD), BF16)


def reorder(head_order, q, k, v, rate):
    whole = pl.BlockSpec((TB, 40 * HD), lambda g, o: (0, 0))
    return pl.pallas_call(
        reorder_kernel,
        grid_spec=pltpu.PrefetchScalarGridSpec(
            num_scalar_prefetch=1,
            grid=(8,),
            in_specs=[whole, whole, whole, pl.BlockSpec((1, 16, HD), lambda g, o: (g, 0, 0))],
            out_specs=[
                pl.BlockSpec((1, KVR, FW), lambda g, o: (g, 0, 0)),
                pl.BlockSpec((1, TB, FW), lambda g, o: (g, 0, 0)),
            ],
        ),
        out_shape=[
            jax.ShapeDtypeStruct((8, KVR, FW), BF16),
            jax.ShapeDtypeStruct((8, TB, FW), BF16),
        ],
        name="reorder",
    )(head_order, q, k, v, rate)


def scatter_kernel(kvr, q, wg, wu, wd, w2, w1, w0, qb, wrec, lkv, lq, lsem, s_kv, s_q, s_f, s_g, s_r, s_w, r_kv, r_q, r_w0, r_w1, r_w):
    row, z, x, c = coords()
    half = lax.div(z, 2)
    block = lax.rem(z, 2) * 4 + x * 2 + c
    own = half == c
    mine = 4 * x + z
    barrier = pltpu.get_barrier_semaphore()
    for zs in (0, 1):
        for xs in (0, 1):
            for cs in (0, 1):
                zz = 2 * c + zs

                @pl.when(jnp.logical_not((zz == z) & (xs == x) & (cs == c)))
                def _():
                    signal(barrier, dev(row, zz, xs, cs))

    @pl.when((c == 0) & (row > 0))
    def _():
        signal(barrier, dev(row - 1, z, x, 0))
        signal(barrier, dev(row - 1, z, x, 1))

    @pl.when(c == 1)
    def _():
        signal(barrier, dev(row, z, x, 0))

    @pl.when(jnp.logical_not(own))
    def _():
        signal(barrier, dev(row, z, x, 1 - c))

    one = lambda p: p.astype(jnp.int32)
    pl.semaphore_wait(barrier, 8 - one(own) + one(row < ROWS - 1) + one(c == 0) + one(own))

    @pl.when(own)
    def _():
        pltpu.make_async_copy(kvr.at[mine], lkv, lsem.at[0]).start()
        pltpu.make_async_copy(q.at[mine], lq, lsem.at[1]).start()

    @pl.when(jnp.logical_not(own))
    def _():
        rcopy(kvr.at[mine], w2.at[block], s_kv.at[7], r_kv.at[block], dev(row, z, x, 1 - c)).start()

    def target(dz, dx):
        zt, xt = lax.rem(z + dz, 4), lax.rem(x + dx, 2)
        return 4 * xt + zt, dev(row, zt, xt, half)

    for n, (dz, dx) in enumerate(SEND_ORDER):
        g, to = target(dz, dx)
        rcopy(kvr.at[g], w2.at[block], s_kv.at[n], r_kv.at[block], to).start()

    @pl.when(own)
    def _():
        for n, w in enumerate((wg, wu, wd)):
            rcopy(w.at[lax.rem(z, 2)], wrec.at[n], s_w.at[n], r_w.at[n], dev(row, z, x, 1 - c)).start()

    for n, (dz, dx) in enumerate(SEND_ORDER):
        g, to = target(dz, dx)
        rcopy(q.at[g], qb.at[block], s_q.at[n], r_q.at[block], to).start()

    @pl.when(jnp.logical_not(own))
    def _():
        rcopy(q.at[mine], qb.at[block], s_q.at[7], r_q.at[block], dev(row, z, x, 1 - c)).start()

    @pl.when(own)
    def _():
        sem_wait_bytes(lkv, lsem.at[0])
        pltpu.make_async_copy(lkv, w2.at[block], r_kv.at[block]).start()
        sem_wait_bytes(lq, lsem.at[1])
        pltpu.make_async_copy(lq, qb.at[block], r_q.at[block]).start()

    for dz, dx in WAIT_ORDER:
        zs, xs = lax.rem(z + 4 - dz, 4), lax.rem(x + dx, 2)

        @pl.when(lax.div(zs, 2) == c)
        def _():
            for cs in (0, 1):
                b = lax.rem(zs, 2) * 4 + xs * 2 + cs
                sem_wait_bytes(w2.at[b], r_kv.at[b])
                kv = w2.at[b, pl.ds(0, 2 * TB)]

                @pl.when((row < ROWS - 1) & (c == 0))
                def _():
                    rcopy(kv, w0.at[b], s_f.at[b], r_w0.at[b], dev(row + 1, z, x, 0)).start()

                @pl.when((row < ROWS - 1) & (c == 1))
                def _():
                    rcopy(kv, w1.at[b], s_f.at[b], r_w1.at[b], dev(row + 1, z, x, 0)).start()

                @pl.when(c == 0)
                def _():
                    rcopy(kv, w1.at[b], s_g.at[b], r_w1.at[b], dev(row, z, x, 1)).start()

    @pl.when((c == 0) & (row > 0))
    def _():
        for dz, dx in WAIT_ORDER:
            zs, xs = lax.rem(z + 4 - dz, 4), lax.rem(x + dx, 2)

            @pl.when(lax.div(zs, 2) == 1)
            def _():
                for cs in (0, 1):
                    b = lax.rem(zs, 2) * 4 + xs * 2 + cs
                    sem_wait_bytes(w1.at[b], r_w1.at[b])
                    rcopy(w1.at[b], w0.at[b], s_r.at[b], r_w0.at[b], dev(row, z, x, 1)).start()

        for b in range(8):
            sem_wait_bytes(w1.at[b], s_r.at[b])

    @pl.when(row > 0)
    def _():
        for b in range(8):
            sem_wait_bytes(w0.at[b], r_w0.at[b])

    @pl.when(c == 1)
    def _():
        for b in range(8):
            sem_wait_bytes(w1.at[b], r_w1.at[b])

    @pl.when(c == 0)
    def _():
        for b in range(8):
            sem_wait_bytes(w1.at[b], s_g.at[b])

    @pl.when(row < ROWS - 1)
    def _():
        for b in range(8):
            sem_wait_bytes(w1.at[b], s_f.at[b])

    for b in range(8):
        sem_wait_bytes(qb.at[b], r_q.at[b])
    for n in range(7):
        sem_wait_bytes(w2.at[n], s_kv.at[n])
        sem_wait_bytes(qb.at[n], s_q.at[n])

    @pl.when(jnp.logical_not(own))
    def _():
        sem_wait_bytes(w2.at[7], s_kv.at[7])
        sem_wait_bytes(qb.at[7], s_q.at[7])
        for n in range(3):
            sem_wait_bytes(wrec.at[n], r_w.at[n])

    @pl.when(own)
    def _():
        for n in range(3):
            sem_wait_bytes(wrec.at[n], s_w.at[n])


def scatter(kvr, q, wg, wu, wd):
    dma = pltpu.SemaphoreType.DMA
    return pl.pallas_call(
        scatter_kernel,
        in_specs=[ANY] * 5,
        out_specs=[ANY] * 5,
        out_shape=[
            jax.ShapeDtypeStruct((8, KVR, FW), BF16),
            jax.ShapeDtypeStruct((8, 2 * TB, FW), BF16),
            jax.ShapeDtypeStruct((8, 2 * TB, FW), BF16),
            jax.ShapeDtypeStruct((8, TB, FW), BF16),
            jax.ShapeDtypeStruct((3, FW, FW), BF16),
        ],
        scratch_shapes=[
            pltpu.VMEM((KVR, FW), BF16),
            pltpu.VMEM((TB, FW), BF16),
            dma((2,)),
        ]
        + [dma((8,))] * 5
        + [dma((3,))]
        + [dma((8,))] * 4
        + [dma((3,))],
        compiler_params=pltpu.CompilerParams(collective_id=0, has_side_effects=True),
        name="scatter",
    )(kvr, q, wg, wu, wd)


def fetch_weights(ws, wrec, wbuf, sem):
    _, z, x, c = coords()

    @pl.when(lax.div(z, 2) == c)
    def _():
        for n in range(3):
            pltpu.make_async_copy(ws[n].at[lax.rem(z, 2)], wbuf.at[n], sem.at[n]).start()

    @pl.when(lax.div(z, 2) != c)
    def _():
        for n in range(3):
            pltpu.make_async_copy(wrec.at[n], wbuf.at[n], sem.at[n]).start()


def dot(a, b, dims):
    return lax.dot_general(a, b, (dims, ((), ())), preferred_element_type=F32)


def normed(x):
    x = x.astype(F32)
    return (x * lax.rsqrt(jnp.mean(x * x, axis=-1, keepdims=True) + 1e-6)).astype(BF16)


def grads_kernel(wg, wu, wd, wrec, w2, grad, wbuf, kn, hid, tgt, bgu, sem):
    fetch_weights((wg, wu, wd), wrec, wbuf, sem)
    for n in range(3):
        sem_wait_bytes(wbuf.at[n], sem.at[n])

    def tile(b, _):
        rows = pl.ds(pl.multiple_of(b * TB, TB), TB)
        k = normed(w2[b, 0:TB, :])
        kn[rows, :] = k
        rate = w2[b, 2 * TB : KVR, 0:HD].astype(F32)[0:1]
        rate = jnp.broadcast_to(rate, (TB, TB)).T
        for j in range(GH):
            at = slice(j * HD, (j + 1) * HD)
            tgt[rows, at] = (rate * w2[b, TB : 2 * TB, at].astype(F32)).astype(BF16)
        pre_gate = dot(k, wbuf[0], ((1,), (0,)))
        pre_up = dot(k, wbuf[1], ((1,), (0,)))
        back = -dot(tgt[rows, :], wbuf[2], ((1,), (1,)))
        sig = jax.nn.sigmoid(pre_gate)
        lifted = pre_gate * sig
        hid[rows, :] = (lifted * pre_up).astype(BF16)
        bgu[rows, 0:FW] = (back * pre_up * sig * (1.0 + pre_gate * (1.0 - sig))).astype(BF16)
        bgu[rows, FW:] = (back * lifted).astype(BF16)
        return 0

    lax.fori_loop(0, 8, tile, 0)

    def out(i, _):
        at = pl.ds(pl.multiple_of(i * HD, HD), HD)
        both = dot(kn[:, at], bgu[...], ((0,), (0,)))
        grad[0, at, :] = both[:, 0:FW].astype(BF16)
        grad[1, at, :] = both[:, FW:].astype(BF16)
        grad[2, at, :] = (-dot(hid[:, at], tgt[...], ((0,), (0,)))).astype(BF16)
        return 0

    lax.fori_loop(0, GH, out, 0)


def grads(wg, wu, wd, wrec, w2):
    return pl.pallas_call(
        grads_kernel,
        in_specs=[ANY] * 4 + [VM],
        out_specs=VM,
        out_shape=jax.ShapeDtypeStruct((3, FW, FW), BF16),
        scratch_shapes=[
            pltpu.VMEM((3, FW, FW), BF16),
            pltpu.VMEM((8 * TB, FW), BF16),
            pltpu.VMEM((8 * TB, FW), BF16),
            pltpu.VMEM((8 * TB, FW), BF16),
            pltpu.VMEM((8 * TB, 2 * FW), BF16),
            pltpu.SemaphoreType.DMA((3,)),
        ],
        name="grads",
    )(wg, wu, wd, wrec, w2)


HALF = FW // 2
PART = FW // 8


def reduce_kernel(grad, out, r0, h, r1, part, r2, s0, t0, s1, t1, s2, t2, s3, t3, s4, t4):
    row, z, x, c = coords()
    y, xh = lax.rem(row, 4), lax.div(row, 4)
    partner = dev(row, z, x, 1 - c)
    across = dev((1 - xh) * 4 + y, z, x, c)
    peer = lambda k: lax.rem(y + k, 4)
    peer_dev = lambda k: dev(xh * 4 + peer(k), z, x, c)
    barrier = pltpu.get_barrier_semaphore()
    signal(barrier, partner)
    signal(barrier, across)
    for k in (1, 2, 3):
        signal(barrier, peer_dev(k))
    pl.semaphore_wait(barrier, 5)
    order = (2, 1, 3, 0)
    rows = lambda core, k: pl.ds(pl.multiple_of(core * HALF + peer(k) * PART, 16), PART)
    for k in order:
        rcopy(grad.at[:, rows(1 - c, k), :], r0.at[peer(k)], s0.at[k], t0.at[peer(k)], partner).start()
    for k in order:
        j = peer(k)
        sem_wait_bytes(r0.at[j], t0.at[j])
        total = grad[:, rows(c, k), :].astype(F32) + r0[j].astype(F32)
        if k:
            h[k] = total.astype(BF16)
            rcopy(h.at[k], r1.at[4 - k], s1.at[k], t1.at[4 - k], peer_dev(k)).start()
    for k in (1, 3, 2):
        sem_wait_bytes(r1.at[k], t1.at[k])
        total = total + r1[k].astype(F32)
    part[0] = total.astype(BF16)
    rcopy(part.at[0], r2, s2, t2, across).start()
    sem_wait_bytes(r2, t2)
    mine = rows(c, 0)
    out[:, mine, :] = (part[0].astype(F32) + r2[...].astype(F32)).astype(BF16)
    for k in (2, 1, 3):
        rcopy(out.at[:, mine, :], out.at[:, mine, :], s3.at[k], t3.at[4 - k], peer_dev(k)).start()
    rcopy(out.at[:, mine, :], out.at[:, mine, :], s4.at[0], t4.at[y], partner).start()
    for k in (1, 3, 2):
        got = out.at[:, rows(c, k), :]
        sem_wait_bytes(r2, t3.at[k])
        rcopy(got, got, s4.at[k], t4.at[peer(k)], partner).start()
    for k in range(4):
        sem_wait_bytes(r2, t4.at[k])
        sem_wait_bytes(r2, s0.at[k])
        sem_wait_bytes(r2, s4.at[k])
        if k:
            sem_wait_bytes(r2, s1.at[k])
            sem_wait_bytes(r2, s3.at[k])
    sem_wait_bytes(r2, s2)


def reduce_grads(grad):
    dma = pltpu.SemaphoreType.DMA
    piece = (3, PART, FW)
    return pl.pallas_call(
        reduce_kernel,
        in_specs=[VM],
        out_specs=VM,
        out_shape=jax.ShapeDtypeStruct((3, FW, FW), BF16),
        scratch_shapes=[
            pltpu.VMEM((4,) + piece, BF16),
            pltpu.VMEM((4,) + piece, BF16),
            pltpu.VMEM((4,) + piece, BF16),
            pltpu.VMEM((1,) + piece, BF16),
            pltpu.VMEM(piece, BF16),
            dma((4,)),
            dma((4,)),
            dma((4,)),
            dma((4,)),
            dma,
            dma,
            dma((4,)),
            dma((4,)),
            dma((4,)),
            dma((4,)),
        ],
        compiler_params=pltpu.CompilerParams(collective_id=1, has_side_effects=True),
        name="reduce",
    )(grad)


TQ = 256
TK = 256
SCALE = HD**-0.5 * 1.4426950408889634


def attend_kernel(order, window, first, q, w0, w1, w2, doc, o, k_all, v_all):
    row, z, x, c = coords()
    head = order[(4 * x + z) * GH + pl.program_id(0)]
    win = window[head]
    start = row * 2048 + c * 1024
    for n, w in enumerate((w0, w1, w2)):
        for b in range(8):
            at = slice(n * 1024 + b * TB, n * 1024 + (b + 1) * TB)
            k_all[at, :] = w[b, 0:TB, :]
            v_all[at, :] = w[b, TB : 2 * TB, :]

    for i in range(1024 // TQ):
        qt = q[2 * i : 2 * i + 2].reshape(TQ, HD)
        pos0 = start + i * TQ
        row_low = jnp.maximum(doc[i * TQ : (i + 1) * TQ, :], pos0 + lax.broadcasted_iota(jnp.int32, (TQ, HD), 0) - win + 1)
        low_first = jnp.maximum(first[i * TQ], pos0 - win + 1)
        low_last = jnp.maximum(first[i * TQ + TQ - 1], pos0 + TQ - win)
        base = start - 2048
        lo = lax.div(low_first - base, TK)
        hi = (2048 + i * TQ) // TK

        def chunk(j, carry, masked):
            m, l, acc = carry
            at = pl.ds(pl.multiple_of(j * TK, TK), TK)
            s = dot(qt, k_all[at, :], ((1,), (1,)))
            if masked:
                kp = base + j * TK + lax.broadcasted_iota(jnp.int32, (TQ, TK), 1)
                qp = pos0 + lax.broadcasted_iota(jnp.int32, (TQ, TK), 0)
                low = jnp.concatenate([row_low] * (TK // HD), axis=1)
                s = jnp.where((kp <= qp) & (kp >= low), s, -1e30)
            m_new = jnp.maximum(m, jnp.max(s, axis=1, keepdims=True))
            p = jnp.exp2((s - m_new) * SCALE)
            if masked:
                p = jnp.where(s > -1e29, p, 0.0)
            a = jnp.exp2((m - m_new) * SCALE)
            l = a * l + jnp.sum(p, axis=1, keepdims=True)
            acc = a * acc + dot(p.astype(BF16), v_all[at, :], ((1,), (0,)))
            return m_new, l, acc

        def step(j, carry):
            whole = base + j * TK >= low_last
            return lax.cond(whole, lambda cr: chunk(j, cr, False), lambda cr: chunk(j, cr, True), carry)

        zero = (jnp.full((TQ, 1), -1e30, F32), jnp.zeros((TQ, 1), F32), jnp.zeros((TQ, HD), F32))
        carry = chunk(hi, zero, True)
        m, l, acc = lax.fori_loop(lo, hi, step, carry)
        o[i * TQ : (i + 1) * TQ, :] = acc / l


def attend(order, window, first, q, w0, w1, w2, doc):
    def lane(rows, depth):
        return pl.BlockSpec((depth, rows, HD), lambda h, *_: (0, 0, h))

    return pl.pallas_call(
        attend_kernel,
        grid_spec=pltpu.PrefetchScalarGridSpec(
            num_scalar_prefetch=3,
            grid=(GH,),
            in_specs=[
                lane(TB, 8),
                lane(2 * TB, 8),
                lane(2 * TB, 8),
                lane(2 * TB, 8),
                pl.BlockSpec((1024, HD), lambda h, *_: (0, 0)),
            ],
            out_specs=pl.BlockSpec((1024, HD), lambda h, *_: (0, h)),
            scratch_shapes=[pltpu.VMEM((3072, HD), BF16), pltpu.VMEM((3072, HD), BF16)],
        ),
        out_shape=jax.ShapeDtypeStruct((1024, FW), F32),
        name="attend",
    )(order, window, first, q, w0, w1, w2, doc)


def apply_kernel(rates, wg, wu, wd, wrec, grad, q, att, o, wbuf, new, sem):
    fetch_weights((wg, wu, wd), wrec, wbuf, sem)
    _, z, x, c = coords()
    rate = rates[4 * x + z]
    for n in range(3):
        sem_wait_bytes(wbuf.at[n], sem.at[n])

        def square(i, s):
            g = grad[n, pl.ds(pl.multiple_of(i * 32, 32), 32), :].astype(F32)
            return s + g * g

        total = lax.fori_loop(0, FW // 32, square, jnp.zeros((32, FW), F32))
        mean = jnp.sum(jnp.sum(total, axis=0, keepdims=True), axis=1, keepdims=True) * (1.0 / (FW * FW))
        factor = rate * lax.rsqrt(mean + 1e-6)

        def column(i, _):
            at = pl.ds(pl.multiple_of(i * HD, HD), HD)
            old = wbuf[n, :, at].astype(F32)
            moved = old - factor * grad[n, :, at].astype(F32)
            kept = jnp.sqrt(jnp.sum(old * old, axis=0, keepdims=True))
            fresh = jnp.sqrt(jnp.sum(moved * moved, axis=0, keepdims=True) + 1e-6)
            new[n, :, at] = (moved * (kept / fresh)).astype(BF16)
            return 0

        lax.fori_loop(0, GH, column, 0)

    def tile(b, _):
        qn = normed(q[b])
        gate = dot(qn, new[0], ((1,), (0,)))
        up = dot(qn, new[1], ((1,), (0,)))
        applied = (gate * jax.nn.sigmoid(gate) * up).astype(BF16)
        out = dot(applied, new[2], ((1,), (0,)))
        rows = pl.ds(pl.multiple_of(b * TB, TB), TB)
        o[b] = (out + att[rows, :]).astype(BF16)
        return 0

    lax.fori_loop(0, 8, tile, 0)


def apply(rates, wg, wu, wd, wrec, grad, q, att):
    return pl.pallas_call(
        apply_kernel,
        in_specs=[pl.BlockSpec(memory_space=pltpu.SMEM)] + [ANY] * 4 + [VM] * 3,
        out_specs=VM,
        out_shape=jax.ShapeDtypeStruct((8, TB, FW), BF16),
        scratch_shapes=[
            pltpu.VMEM((3, FW, FW), BF16),
            pltpu.VMEM((3, FW, FW), BF16),
            pltpu.SemaphoreType.DMA((3,)),
        ],
        name="apply",
    )(rates, wg, wu, wd, wrec, grad, q, att)


def gather_kernel(a, out, buf, lsem, ssem, rsem):
    row, z, x, c = coords()
    half = lax.div(z, 2)
    own = half == c
    mine = 4 * x + z
    block = lax.rem(z, 2) * 4 + x * 2 + c
    barrier = pltpu.get_barrier_semaphore()

    for dz in range(4):
        for dx in range(2):
            zs, xs = lax.rem(z + dz, 4), lax.rem(x + dx, 2)
            if (dz, dx) == (0, 0):

                @pl.when(jnp.logical_not(own))
                def _():
                    signal(barrier, dev(row, zs, xs, half))
            else:
                signal(barrier, dev(row, zs, xs, half))
    pl.semaphore_wait(barrier, 8 - own.astype(jnp.int32))

    @pl.when(own)
    def _():
        pltpu.make_async_copy(a.at[block], buf, lsem).start()

    order = ((0, 1), (1, 0), (1, 1), (3, 0), (3, 1), (2, 0), (2, 1), (0, 0))
    for dz, dx in order:
        zt, xt = lax.rem(z + dz, 4), lax.rem(x + dx, 2)

        @pl.when(lax.div(zt, 2) == c)
        def _():
            for ct in (0, 1):
                b = lax.rem(zt, 2) * 4 + xt * 2 + ct
                if (dz, dx) == (0, 0):

                    @pl.when(ct != c)
                    def _():
                        rcopy(a.at[b], out.at[mine], ssem.at[b], rsem.at[mine], dev(row, zt, xt, ct)).start()
                else:
                    rcopy(a.at[b], out.at[mine], ssem.at[b], rsem.at[mine], dev(row, zt, xt, ct)).start()

    @pl.when(own)
    def _():
        sem_wait_bytes(buf, lsem)
        pltpu.make_async_copy(buf, out.at[mine], rsem.at[mine]).start()

    for g in range(8):
        sem_wait_bytes(buf, rsem.at[g])
    for b in range(8):

        @pl.when(jnp.logical_not(own & (block == b)))
        def _():
            sem_wait_bytes(buf, ssem.at[b])


def gather(a):
    dma = pltpu.SemaphoreType.DMA
    return pl.pallas_call(
        gather_kernel,
        in_specs=[ANY],
        out_specs=ANY,
        out_shape=jax.ShapeDtypeStruct((8, TB, FW), BF16),
        scratch_shapes=[pltpu.VMEM((TB, FW), BF16), dma, dma((8,)), dma((8,))],
        compiler_params=pltpu.CompilerParams(collective_id=2, has_side_effects=True),
        name="gather",
    )(a)


def restore_kernel(order, a, o):
    for g in range(8):
        for j in range(GH):
            at = pl.ds(pl.multiple_of(order[g * GH + j] * HD, HD), HD)
            o[:, at] = a[g, :, j * HD : (j + 1) * HD]


def restore(order, a):
    return pl.pallas_call(
        restore_kernel,
        grid_spec=pltpu.PrefetchScalarGridSpec(
            num_scalar_prefetch=1,
            grid=(4,),
            in_specs=[pl.BlockSpec((8, TB // 4, FW), lambda i, o: (0, i, 0))],
            out_specs=pl.BlockSpec((TB // 4, 40 * HD), lambda i, o: (i, 0)),
        ),
        out_shape=jax.ShapeDtypeStruct((TB, 40 * HD), BF16),
        name="restore",
    )(order, a)


def per_device(queries, keys, values, step_rate, doc_start, window_len, head_order, learn_rate, w_gate, w_up, w_down):
    rate = jnp.broadcast_to(step_rate.T[:, None, :], (8, 16, TB))
    kvr, q = reorder(head_order, queries, keys, values, rate)
    w2, w1, w0, qb, wrec = scatter(kvr, q, w_gate, w_up, w_down)
    c = lax.rem(lax.axis_index("head"), 2)
    row = lax.div(lax.axis_index("seq"), 4)
    first = lax.dynamic_slice_in_dim(doc_start, row * 2048 + c * 1024, 1024)
    doc = jnp.broadcast_to(first[:, None], (1024, HD))
    grad = reduce_grads(grads(w_gate, w_up, w_down, wrec, w2))
    att = attend(head_order, window_len, first, qb, w0, w1, w2, doc)
    mixed = apply(learn_rate, w_gate, w_up, w_down, wrec, grad, qb, att)
    return restore(head_order, gather(mixed))


def solution(mesh):
    both = P(("seq", "head"), None)
    placed = (both, both, both, both, P(), P(), P(), P()) + (P("head", None, None),) * 3
    return jax.shard_map(per_device, mesh=mesh, in_specs=placed, out_specs=both, check_vma=False)
```

time: 706 us -> 374 us (0.53)
  waiting for transfers between devices: 406 us -> 0 us
  Pallas kernels: 0 us -> 272 us
  local copies, waits for them, and re-layouts: 104 us -> 2.32 us
  blocking collectives: 0 us -> 94.3 us
  matrix products: 92.5 us -> 0 us
  other arithmetic: 50.5 us -> 0 us
  starting transfers between devices: 30.4 us -> 0 us
  between operations: 14.4 us -> 0.04 us
    pallas_call x0 -> x8, Pallas kernels: none -> 272 us  [the longest x1 112 us: scatter(): pl.pallas_call(scatter_kernel, in_specs=[ANY] * 5, out_specs=[ANY] * 5, o...]
    psum x1 -> x0, waiting for transfers between devices: 201 us -> none  [per_device(): lax.psum(grad_down.astype(jnp.bfloat16), 'seq').astype(jnp.float32)]
    ppermute x4 -> x0, waiting for transfers between devices: 172 us -> none  [passed_along(): return lax.ppermute(x, axis, pairs)]
    unnamed x0 -> x1, blocking collectives: none -> 94.3 us
    dot_general x28 -> x0, matrix products: 92.5 us -> none  [the longest x10 38.3 us: attend(): return jnp.dot(weights_bf, value_block, preferred_element_type=jnp.float32)]
    all_to_all x5 -> x0, waiting for transfers between devices: 32.6 us -> none  [the longest x1 16.3 us: per_device(): lax.all_to_all(summed_out, 'head', split_axis=0, concat_axis=1, tiled=True)]
    reduce_sum x18 -> x0, other arithmetic: 31.6 us -> none  [the longest x10 22 us: attend(): jnp.sum(weights, axis=1, keepdims=True)]
    slice x3 -> x0, local copies, waits for them, and re-layouts: 24.1 us -> none  [the longest x2 14.5 us: per_device(): buffer[1].reshape(WINDOW + group_rows, local_heads, head_size)]
  transfers between devices with their start and end apart: 10 -> 0, of which waited for: 7 -> 0; matrix products, arithmetic and copies ran while one was open for 12% -> 0% of each run, Pallas kernels for 0% -> 0%
where the time goes in v1:
time: 374 us; the launch traced here: 369 us
  Pallas kernels  272 us (73%)
  blocking collectives  94.3 us (25%)
    pallas_call x1, Pallas kernels, scatter(): pl.pallas_call(scatter_kernel, in_specs=[ANY] * 5, out_specs=[ANY] * 5, o...  112 us
    unnamed x1, blocking collectives  94.3 us
    pallas_call x1, Pallas kernels, reduce_grads(): pl.pallas_call(reduce_kernel, in_specs=[VM], out_specs=VM, out_shape=jax....  64.6 us
    pallas_call x1, Pallas kernels, attend(): pl.pallas_call(attend_kernel, grid_spec=pltpu.PrefetchScalarGridSpec(num_...  34.2 us
    pallas_call x1, Pallas kernels, gather(): pl.pallas_call(gather_kernel, in_specs=[ANY], out_specs=ANY, out_shape=ja...  19.6 us
    pallas_call x1, Pallas kernels, grads(): pl.pallas_call(grads_kernel, in_specs=[ANY] * 4 + [VM], out_specs=VM, out...  15.2 us
    pallas_call x1, Pallas kernels, apply(): pl.pallas_call(apply_kernel, in_specs=[pl.BlockSpec(memory_space=pltpu.SM...  14.8 us

profile of v1, /device:TPU:4, one launch (start us, length us, event | category | flops | bytes accessed | tf_op | source)
XLA Modules:
  0.0 368.8 jit_solution(1276867303670406280)
XLA Ops:
  0.0 1.3 broadcast_in_dim.4.rate
  1.3 94.3 %all-gather.1 = s32[32,1,512]{2,1,0:T(1,128)S(1)} all-gather(s32[1,1,512]{2,1,0:T(1,128)} %bitcast.5), channel_id=1, replica_groups=mesh['seq'=32,'head'=4] {'seq'}, dimensions={0}, use_global_device_ids=true | all-gather | bytes 67584 | tf_op args[4]
  95.6 0.0 copy-start
  95.6 1.0 broadcast_in_dim.5.doc
  96.6 7.2 %reorder.1 = (bf16[8,272,640]{2,1,0:T(8,128)(2,1)}, bf16[8,128,640]{2,1,0:T(8,128)(2,1)}) custom-call(s32[40]{0:T(128)} %order.5, bf16[128,5120]{1,0:T(8,128)(2,1)} %q.1, bf16[128,5120]{1,0:T(8,128)(2,1)} %k.1, bf16[128,5120]{1,0:T(8,128)(2,1)} %v.1, bf16[8,16,128]{2,1,0:T(8,128)(2,1)} %broadcast_in_dim.4.rate), custom_call_target="tpu_custom_call" | custom-call | tf_op jit(solution)/shard_map/reorder/pallas_call | solution.py:63
  103.7 0.0 copy-done
  103.7 112.3 %scatter.1 = (bf16[8,272,640]{2,1,0:T(8,128)(2,1)}, bf16[8,256,640]{2,1,0:T(8,128)(2,1)}, bf16[8,256,640]{2,1,0:T(8,128)(2,1)}, bf16[8,128,640]{2,1,0:T(8,128)(2,1)}, bf16[3,640,640]{2,1,0:T(8,128)(2,1)}) custom-call(bf16[8,272,640]{2,1,0:T(8,128)(2,1)} %get-tuple-element.12.kvr, bf16[8,128,640]{2,1,0:T(8,128)(2,1)} %get-tuple-element.13.q, ...), custom_call_target="tpu_custom_call" | custom-call | tf_op jit(solution)/shard_map/scatter/pallas_call | solution.py:229
  216.0 34.2 %attend.1.att = f32[1024,640]{1,0:T(8,128)} custom-call(s32[40]{0:T(128)} %order.5, s32[40]{0:T(128)} %window.1, s32[1024]{0:T(1024)} %copy-done, bf16[8,128,640]{2,1,0:T(8,128)(2,1)} %get-tuple-element.16.q, bf16[8,256,640]{2,1,0:T(8,128)(2,1)} %get-tuple-element.17.w0, bf16[8,256,640]{2,1,0:T(8,128)(2,1)} %get-tuple-element.18.w1, ...), custom_call_target="tpu_custom_call" | custom-call | tf_op jit(solution)/shard_map/attend/pallas_call | solution.py:473
  250.2 15.2 %grads.1.grad = bf16[3,640,640]{2,1,0:T(8,128)(2,1)} custom-call(bf16[2,640,640]{2,1,0:T(8,128)(2,1)} %wg.5, bf16[2,640,640]{2,1,0:T(8,128)(2,1)} %wu.5, bf16[2,640,640]{2,1,0:T(8,128)(2,1)} %wd.5, bf16[3,640,640]{2,1,0:T(8,128)(2,1)} %get-tuple-element.14.wrec, bf16[8,272,640]{2,1,0:T(8,128)(2,1)} %get-tuple-element.15.w2), custom_call_target="tpu_custom_call" | custom-call | tf_op jit(solution)/shard_map/grads/pallas_call | solution.py:315
  265.5 64.6 %reduce.1.grad = bf16[3,640,640]{2,1,0:T(8,128)(2,1)} custom-call(bf16[3,640,640]{2,1,0:T(8,128)(2,1)} %grads.1.grad), custom_call_target="tpu_custom_call" | custom-call | tf_op jit(solution)/shard_map/reduce/pallas_call | solution.py:388
  330.1 14.8 %apply.1.a = bf16[8,128,640]{2,1,0:T(8,128)(2,1)} custom-call(f32[8]{0:T(128)} %rates.1, bf16[2,640,640]{2,1,0:T(8,128)(2,1)} %wg.5, bf16[2,640,640]{2,1,0:T(8,128)(2,1)} %wu.5, bf16[2,640,640]{2,1,0:T(8,128)(2,1)} %wd.5, bf16[3,640,640]{2,1,0:T(8,128)(2,1)} %get-tuple-element.14.wrec, bf16[3,640,640]{2,1,0:T(8,128)(2,1)} %reduce.1.grad, ...), custom_call_target="tpu_custom_call" | custom-call | tf_op jit(solution)/shard_map/apply/pallas_call | solution.py:533
  344.9 19.6 %gather.1.a = bf16[8,128,640]{2,1,0:T(8,128)(2,1)} custom-call(bf16[8,128,640]{2,1,0:T(8,128)(2,1)} %apply.1.a), custom_call_target="tpu_custom_call" | custom-call | tf_op jit(solution)/shard_map/gather/pallas_call | solution.py:603
  364.6 4.2 %restore.1 = bf16[128,5120]{1,0:T(8,128)(2,1)} custom-call(s32[40]{0:T(128)} %order.5, bf16[8,128,640]{2,1,0:T(8,128)(2,1)} %gather.1.a), custom_call_target="tpu_custom_call" | custom-call | tf_op jit(solution)/shard_map/restore/pallas_call | solution.py:622
  (1 shorter events, 0.0 us)
Async XLA Ops:
  95.6 8.2 %copy-start = (s32[1024]{0:T(1024)}, s32[1024]{0:T(1024)S(1)}, u32[]{:S(2)}) copy-start(s32[1024]{0:T(1024)S(1)} %dynamic_slice.3.first) | copy-start | bytes 12292

commit v2 on v0

v2 whole, which is shorter than its diff:
```python
import functools

import jax
import jax.numpy as jnp
from jax import lax
from jax.experimental import pallas as pl
from jax.experimental.pallas import tpu as pltpu
from jax.sharding import PartitionSpec as P

MESH = pl.DeviceIdType.MESH
ANY = pl.BlockSpec(memory_space=pl.ANY)
VM = pl.BlockSpec(memory_space=pltpu.VMEM)
HD = 128
GH = 5
FW = 640
TB = 128
KVR = 272
ROWS = 8
F32 = jnp.float32
BF16 = jnp.bfloat16

SEND_ORDER = ((0, 1), (1, 0), (3, 0), (1, 1), (3, 1), (2, 0), (2, 1))


def coords():
    s, h = lax.axis_index("seq"), lax.axis_index("head")
    return lax.div(s, 4), lax.rem(s, 4), lax.div(h, 2), lax.rem(h, 2)


def dev(row, z, x, c):
    return (row * 4 + z, x * 2 + c)


def sem_wait_bytes(ref, sem):
    pltpu.make_async_copy(ref, ref, sem).wait()


def signal(sem, device):
    pl.semaphore_signal(sem, inc=1, device_id=device, device_id_type=MESH)


def rcopy(src, dst, ssem, rsem, device):
    return pltpu.make_async_remote_copy(
        src_ref=src, dst_ref=dst, send_sem=ssem, recv_sem=rsem, device_id=device, device_id_type=MESH
    )


def reorder_kernel(order, q, k, v, rate, kvr, qo):
    g = pl.program_id(0)
    for j in range(GH):
        at = pl.ds(pl.multiple_of(order[g * GH + j] * HD, HD), HD)
        to = slice(j * HD, (j + 1) * HD)
        kvr[0, 0:TB, to] = k[:, at]
        kvr[0, TB : 2 * TB, to] = v[:, at]
        qo[0, :, to] = q[:, at]
    kvr[0, 2 * TB :, 0:HD] = rate[0]
    kvr[0, 2 * TB :, HD:] = jnp.zeros((KVR - 2 * TB, FW - HD), BF16)


def reorder(head_order, q, k, v, rate):
    whole = pl.BlockSpec((TB, 40 * HD), lambda g, o: (0, 0))
    return pl.pallas_call(
        reorder_kernel,
        grid_spec=pltpu.PrefetchScalarGridSpec(
            num_scalar_prefetch=1,
            grid=(8,),
            in_specs=[whole, whole, whole, pl.BlockSpec((1, 16, HD), lambda g, o: (g, 0, 0))],
            out_specs=[
                pl.BlockSpec((1, KVR, FW), lambda g, o: (g, 0, 0)),
                pl.BlockSpec((1, TB, FW), lambda g, o: (g, 0, 0)),
            ],
        ),
        out_shape=[
            jax.ShapeDtypeStruct((8, KVR, FW), BF16),
            jax.ShapeDtypeStruct((8, TB, FW), BF16),
        ],
        name="reorder",
    )(head_order, q, k, v, rate)

SCALE = HD**-0.5 * 1.4426950408889634
TQ = 256
TK = 512
HALF = FW // 2
PART = FW // 8
LOW = -1e30


def dot(a, b, dims):
    return lax.dot_general(a, b, (dims, ((), ())), preferred_element_type=F32)


def normed(x):
    x = x.astype(F32)
    return (x * lax.rsqrt(jnp.mean(x * x, axis=-1, keepdims=True) + 1e-6)).astype(BF16)


def column(row):
    return jnp.broadcast_to(row, (TB, TB)).T


def layer_kernel(
    kvr, q, wg, wu, wd, rates, wins, out,
    w2, w1, w0, qb, wb, kn, hid, tgt, bgu, grad, r0, h, r1, tot, part, r2, gsum, new, docs, kh, vh, ms, ls, accs, att, mixed,
    s_l, s_kv, s_q, s_f, s_g, s_r, s_w, r_kv, r_q, r_w0, r_w1, r_w, s0, t0, s1, t1, s2, t2, s3, t3, s4, t4, s_o, r_o,
):
    row, z, x, c = coords()
    half = lax.div(z, 2)
    block = lax.rem(z, 2) * 4 + x * 2 + c
    own = half == c
    mine = 4 * x + z
    y, xh = lax.rem(row, 4), lax.div(row, 4)
    partner = dev(row, z, x, 1 - c)
    across = dev((1 - xh) * 4 + y, z, x, c)
    peer = lambda k: lax.rem(y + k, 4)
    peer_dev = lambda k: dev(xh * 4 + peer(k), z, x, c)
    last = row == ROWS - 1
    one = lambda p: p.astype(jnp.int32)

    barrier = pltpu.get_barrier_semaphore()
    for dz in range(4):
        for dx in range(2):
            for dc in range(2):
                if dz or dx or dc:
                    signal(barrier, dev(row, lax.rem(z + dz, 4), lax.rem(x + dx, 2), lax.rem(c + dc, 2)))
    for k in (1, 2, 3):
        signal(barrier, peer_dev(k))
    signal(barrier, across)

    @pl.when((c == 0) & (row > 0))
    def _():
        signal(barrier, dev(row - 1, z, x, 0))
        signal(barrier, dev(row - 1, z, x, 1))

    @pl.when(own)
    def _():
        pltpu.make_async_copy(kvr.at[mine], w2.at[block], r_kv.at[block]).start()
        pltpu.make_async_copy(q.at[mine], qb.at[block], r_q.at[block]).start()
        for n, w in enumerate((wg, wu, wd)):
            pltpu.make_async_copy(w.at[lax.rem(z, 2)], wb.at[n], r_w.at[n]).start()

    @pl.when(row == 0)
    def _():
        w0[...] = jnp.zeros_like(w0)

    @pl.when((row == 0) & (c == 0))
    def _():
        w1[...] = jnp.zeros_like(w1)

    pl.semaphore_wait(barrier, 19 + one(jnp.logical_not(last)))

    def target(dz, dx):
        zt, xt = lax.rem(z + dz, 4), lax.rem(x + dx, 2)
        return 4 * xt + zt, dev(row, zt, xt, half)

    @pl.when(jnp.logical_not(own))
    def _():
        rcopy(kvr.at[mine], w2.at[block], s_kv.at[7], r_kv.at[block], partner).start()

    for n, (dz, dx) in enumerate(SEND_ORDER):
        g, to = target(dz, dx)
        rcopy(kvr.at[g], w2.at[block], s_kv.at[n], r_kv.at[block], to).start()

    @pl.when(own)
    def _():
        for n, w in enumerate((wg, wu, wd)):
            rcopy(w.at[lax.rem(z, 2)], wb.at[n], s_w.at[n], r_w.at[n], partner).start()

    for n, (dz, dx) in enumerate(SEND_ORDER):
        g, to = target(dz, dx)
        rcopy(q.at[g], qb.at[block], s_q.at[n], r_q.at[block], to).start()

    @pl.when(jnp.logical_not(own))
    def _():
        rcopy(q.at[mine], qb.at[block], s_q.at[7], r_q.at[block], partner).start()

    for n in range(3):
        sem_wait_bytes(wb.at[n], r_w.at[n])

    near = jnp.where(own, lax.rem(z, 2), jnp.where(z == 0, 1, jnp.where(z == 3, 0, 1 - lax.rem(z, 2))))

    def nth(n, z_first):
        zs = lax.rem(z_first + lax.div(n, 4), 2)
        xs = lax.rem(x + lax.rem(lax.div(n, 2), 2), 2)
        return zs * 4 + xs * 2 + lax.rem(n, 2)

    def arrive(n, _):
        b = nth(n, near)
        sem_wait_bytes(w2.at[b], r_kv.at[b])
        kv = w2.at[b, pl.ds(0, 2 * TB)]

        @pl.when(jnp.logical_not(last) & (c == 0))
        def _():
            rcopy(kv, w0.at[b], s_f.at[b], r_w0.at[b], dev(row + 1, z, x, 0)).start()

        @pl.when(jnp.logical_not(last) & (c == 1))
        def _():
            rcopy(kv, w1.at[b], s_f.at[b], r_w1.at[b], dev(row + 1, z, x, 0)).start()

        @pl.when(c == 0)
        def _():
            rcopy(kv, w1.at[b], s_g.at[b], r_w1.at[b], partner).start()

        rows = pl.ds(pl.multiple_of(b * TB, TB), TB)
        k = normed(w2[b, 0:TB, :])
        kn[rows, :] = k
        extra = w2[b, 2 * TB : KVR, 0:HD].astype(F32)
        docs[rows, :] = column(extra[1:2]) * float(TB) + column(extra[2:3])
        rate = column(extra[0:1])
        for j in range(GH):
            at = slice(j * HD, (j + 1) * HD)
            tgt[rows, at] = (rate * w2[b, TB : 2 * TB, at].astype(F32)).astype(BF16)
        pre_gate = dot(k, wb[0], ((1,), (0,)))
        pre_up = dot(k, wb[1], ((1,), (0,)))
        back = -dot(tgt[rows, :], wb[2], ((1,), (1,)))
        sig = jax.nn.sigmoid(pre_gate)
        lifted = pre_gate * sig
        hid[rows, :] = (lifted * pre_up).astype(BF16)
        bgu[rows, 0:FW] = (back * pre_up * sig * (1.0 + pre_gate * (1.0 - sig))).astype(BF16)
        bgu[rows, FW:] = (back * lifted).astype(BF16)
        return 0

    lax.fori_loop(0, 8, arrive, 0)

    def grad_rows(i, _):
        at = pl.ds(pl.multiple_of(i * HD, HD), HD)
        both = dot(kn[:, at], bgu[...], ((0,), (0,)))
        grad[0, at, :] = both[:, 0:FW].astype(BF16)
        grad[1, at, :] = both[:, FW:].astype(BF16)
        grad[2, at, :] = (-dot(hid[:, at], tgt[...], ((0,), (0,)))).astype(BF16)
        return 0

    lax.fori_loop(0, GH, grad_rows, 0)

    rows_of = lambda core, k: pl.ds(pl.multiple_of(core * HALF + peer(k) * PART, 16), PART)
    order = (2, 1, 3, 0)
    for k in order:
        rcopy(grad.at[:, rows_of(1 - c, k), :], r0.at[k], s0.at[k], t0.at[k], partner).start()
    for k in order:
        sem_wait_bytes(r0.at[k], t0.at[k])
        total = grad[:, rows_of(c, k), :].astype(F32) + r0[k].astype(F32)
        if k:
            h[k] = total.astype(BF16)
            rcopy(h.at[k], r1.at[4 - k], s1.at[k], t1.at[4 - k], peer_dev(k)).start()
        else:
            tot[...] = total

    def reduce_y():
        for k in (1, 3, 2):
            sem_wait_bytes(r1.at[k], t1.at[k])
        total = tot[...] + r1[1].astype(F32) + r1[2].astype(F32) + r1[3].astype(F32)
        part[...] = total.astype(BF16)
        rcopy(part, r2, s2, t2, across).start()

    def reduce_x():
        sem_wait_bytes(r2, t2)
        at = rows_of(c, 0)
        gsum[:, at, :] = (part[...].astype(F32) + r2[...].astype(F32)).astype(BF16)
        done = gsum.at[:, at, :]
        for k in (2, 1, 3):
            rcopy(done, done, s3.at[k], t3.at[4 - k], peer_dev(k)).start()
        rcopy(done, done, s4.at[0], t4.at[y], partner).start()

    def reduce_end():
        for k in (1, 3, 2):
            got = gsum.at[:, rows_of(c, k), :]
            sem_wait_bytes(r2, t3.at[k])
            rcopy(got, got, s4.at[k], t4.at[peer(k)], partner).start()
        for k in range(4):
            sem_wait_bytes(r2, t4.at[k])

    @pl.when((c == 0) & (row > 0))
    def _():
        def relay(n, _):
            b = nth(n, jnp.where(half == 1, lax.rem(z, 2), 1 - z))
            sem_wait_bytes(w1.at[b], r_w1.at[b])
            rcopy(w1.at[b], w0.at[b], s_r.at[b], r_w0.at[b], partner).start()
            return 0

        lax.fori_loop(0, 8, relay, 0)

    @pl.when(row > 0)
    def _():
        for b in range(8):
            sem_wait_bytes(w0.at[b], r_w0.at[b])

    @pl.when(c == 1)
    def _():
        for b in range(8):
            sem_wait_bytes(w1.at[b], r_w1.at[b])

    for b in range(8):
        sem_wait_bytes(qb.at[b], r_q.at[b])

    base = (row * 2048 + c * 1024 - 2048).astype(F32)
    lane = lax.broadcasted_iota(jnp.int32, (TQ, HD), 1).astype(F32)
    down = lax.broadcasted_iota(jnp.int32, (TQ, HD), 0).astype(F32)

    def head(hh, _):
        at = pl.ds(pl.multiple_of(hh * HD, HD), HD)
        win = wins[mine * GH + hh].astype(F32)
        for n, w in enumerate((w0, w1, w2)):
            for b in range(8):
                rows = slice(n * 1024 + b * TB, n * 1024 + (b + 1) * TB)
                kh[rows, :] = w[b, 0:TB, at]
                vh[rows, :] = w[b, TB : 2 * TB, at]

        def chunk(i, first, width, start):
            keys = pl.ds(first if isinstance(first, int) else pl.multiple_of(first, TQ), width)
            qt = qb[2 * i : 2 * i + 2, :, at].reshape(TQ, HD)
            s = dot(qt, kh[keys, :], ((1,), (1,)))
            off = first.astype(F32) if not isinstance(first, int) else float(first)
            low = jnp.maximum(docs[i * TQ : (i + 1) * TQ, :] - base, down + (2049.0 + TQ * i) - win) - off
            parts = []
            for t in range(width // HD):
                seen = lane >= low - float(HD * t)
                if start:
                    seen = seen & (lane <= down + float(width - TQ - HD * t))
                parts.append(jnp.where(seen, s[:, t * HD : (t + 1) * HD], LOW))
            top = functools.reduce(jnp.maximum, parts)
            top = jnp.broadcast_to(jnp.max(top, axis=1, keepdims=True), (TQ, HD))
            if not start:
                before = ms[i]
                top = jnp.maximum(before, top)
            ms[i] = top
            ps = [jnp.exp2((p - top) * SCALE) for p in parts]
            total = functools.reduce(jnp.add, ps)
            got = dot(jnp.concatenate([p.astype(BF16) for p in ps], axis=1), vh[keys, :], ((1,), (0,)))
            if start:
                ls[i] = total
                accs[i] = got
            else:
                a = jnp.exp2((before - top) * SCALE)
                ls[i] = a * ls[i] + total
                accs[i] = a * accs[i] + got

        for i in range(4):
            chunk(i, 1792 + TQ * i, TK, True)

        def back(r, _):
            for i in range(4):
                chunk(i, 1792 + TQ * i - TK * r, TK, False)
            return 0

        lax.fori_loop(1, 4, back, 0)
        for i in range(4):
            chunk(i, TQ * i, TQ, False)
            att[i * TQ : (i + 1) * TQ, at] = accs[i] / jnp.sum(ls[i], axis=1, keepdims=True)

        @pl.when(hh == 1)
        def _():
            reduce_y()

        @pl.when(hh == 3)
        def _():
            reduce_x()

        return 0

    lax.fori_loop(0, GH, head, 0)
    reduce_end()

    speed = rates[mine]
    for n in range(3):

        def square(i, s):
            g = gsum[n, pl.ds(pl.multiple_of(i * 32, 32), 32), :].astype(F32)
            return s + g * g

        total = lax.fori_loop(0, FW // 32, square, jnp.zeros((32, FW), F32))
        mean = jnp.sum(jnp.sum(total, axis=0, keepdims=True), axis=1, keepdims=True) * (1.0 / (FW * FW))
        factor = speed * lax.rsqrt(mean + 1e-6)

        def move(i, _):
            at = pl.ds(pl.multiple_of(i * HD, HD), HD)
            old = wb[n, :, at].astype(F32)
            moved = old - factor * gsum[n, :, at].astype(F32)
            kept = jnp.sqrt(jnp.sum(old * old, axis=0, keepdims=True))
            fresh = jnp.sqrt(jnp.sum(moved * moved, axis=0, keepdims=True) + 1e-6)
            new[n, :, at] = (moved * (kept / fresh)).astype(BF16)
            return 0

        lax.fori_loop(0, GH, move, 0)

    def tile(n, _):
        b = nth(7 - n, near)
        qn = normed(qb[b])
        gate = dot(qn, new[0], ((1,), (0,)))
        up = dot(qn, new[1], ((1,), (0,)))
        applied = (gate * jax.nn.sigmoid(gate) * up).astype(BF16)
        rows = pl.ds(pl.multiple_of(b * TB, TB), TB)
        mixed[b] = (dot(applied, new[2], ((1,), (0,))) + att[rows, :]).astype(BF16)
        zt, xt, ct = 2 * c + lax.div(b, 4), lax.rem(lax.div(b, 2), 2), lax.rem(b, 2)
        here = own & (b == block)

        @pl.when(here)
        def _():
            pltpu.make_async_copy(mixed.at[b], out.at[mine], r_o.at[mine]).start()

        @pl.when(jnp.logical_not(here))
        def _():
            rcopy(mixed.at[b], out.at[mine], s_o.at[b], r_o.at[mine], dev(row, zt, xt, ct)).start()

        return 0

    lax.fori_loop(0, 8, tile, 0)
    for g in range(8):
        sem_wait_bytes(mixed.at[g], r_o.at[g])

    for b in range(8):

        @pl.when(jnp.logical_not(own & (block == b)))
        def _():
            sem_wait_bytes(mixed.at[b], s_o.at[b])

    for n in range(7):
        sem_wait_bytes(w2.at[n], s_kv.at[n])
        sem_wait_bytes(qb.at[n], s_q.at[n])

    @pl.when(jnp.logical_not(own))
    def _():
        sem_wait_bytes(w2.at[7], s_kv.at[7])
        sem_wait_bytes(qb.at[7], s_q.at[7])

    @pl.when(own)
    def _():
        for n in range(3):
            sem_wait_bytes(wb.at[n], s_w.at[n])

    @pl.when(c == 0)
    def _():
        for b in range(8):
            sem_wait_bytes(w1.at[b], s_g.at[b])

    @pl.when((c == 0) & (row > 0))
    def _():
        for b in range(8):
            sem_wait_bytes(w1.at[b], s_r.at[b])

    @pl.when(jnp.logical_not(last))
    def _():
        for b in range(8):
            sem_wait_bytes(w1.at[b], s_f.at[b])

    for k in range(4):
        sem_wait_bytes(r2, s0.at[k])
        sem_wait_bytes(r2, s4.at[k])
        if k:
            sem_wait_bytes(r2, s1.at[k])
            sem_wait_bytes(r2, s3.at[k])
    sem_wait_bytes(r2, s2)


def layer(kvr, q, wg, wu, wd, rates, wins):
    dma = pltpu.SemaphoreType.DMA
    piece = (3, PART, FW)
    mats = (3, FW, FW)
    half = (8 * TB, FW)
    vmem = [
        ((8, KVR, FW), BF16),
        ((8, 2 * TB, FW), BF16),
        ((8, 2 * TB, FW), BF16),
        ((8, TB, FW), BF16),
        (mats, BF16),
        (half, BF16),
        (half, BF16),
        (half, BF16),
        ((8 * TB, 2 * FW), BF16),
        (mats, BF16),
        ((4,) + piece, BF16),
        ((4,) + piece, BF16),
        ((4,) + piece, BF16),
        (piece, F32),
        (piece, BF16),
        (piece, BF16),
        (mats, BF16),
        (mats, BF16),
        ((8 * TB, HD), F32),
        ((3072, HD), BF16),
        ((3072, HD), BF16),
        ((4, TQ, HD), F32),
        ((4, TQ, HD), F32),
        ((4, TQ, HD), F32),
        (half, F32),
        ((8, TB, FW), BF16),
    ]
    d4, d8, d3 = dma((4,)), dma((8,)), dma((3,))
    sems = [d3, d8, d8, d8, d8, d8, d3, d8, d8, d8, d8, d3, d4, d4, d4, d4, dma, dma, d4, d4, d4, d4, d8, d8]
    smem = pl.BlockSpec(memory_space=pltpu.SMEM)
    return pl.pallas_call(
        layer_kernel,
        in_specs=[ANY] * 5 + [smem] * 2,
        out_specs=ANY,
        out_shape=jax.ShapeDtypeStruct((8, TB, FW), BF16),
        scratch_shapes=[pltpu.VMEM(s, d) for s, d in vmem] + sems,
        compiler_params=pltpu.CompilerParams(
            collective_id=0, has_side_effects=True, vmem_limit_bytes=60 * 1024 * 1024
        ),
        name="layer",
    )(kvr, q, wg, wu, wd, rates, wins)


def restore_kernel(order, a, o):
    for g in range(8):
        for j in range(GH):
            at = pl.ds(pl.multiple_of(order[g * GH + j] * HD, HD), HD)
            o[:, at] = a[g, :, j * HD : (j + 1) * HD]


def restore(order, a):
    return pl.pallas_call(
        restore_kernel,
        grid_spec=pltpu.PrefetchScalarGridSpec(
            num_scalar_prefetch=1,
            grid=(4,),
            in_specs=[pl.BlockSpec((8, TB // 4, FW), lambda i, o: (0, i, 0))],
            out_specs=pl.BlockSpec((TB // 4, 40 * HD), lambda i, o: (i, 0)),
        ),
        out_shape=jax.ShapeDtypeStruct((TB, 40 * HD), BF16),
        name="restore",
    )(order, a)


def per_device(queries, keys, values, step_rate, doc_start, window_len, head_order, learn_rate, w_gate, w_up, w_down):
    doc = lax.dynamic_slice_in_dim(doc_start, lax.axis_index("head") * TB, TB)
    line = lax.broadcasted_iota(jnp.int32, (8, 16, TB), 1)
    digits = jnp.where(line == 1, (doc // TB)[None, None, :], (doc % TB)[None, None, :]).astype(BF16)
    extra = jnp.where(line == 0, step_rate.T[:, None, :], digits)
    kvr, q = reorder(head_order, queries, keys, values, extra)
    mixed = layer(kvr, q, w_gate, w_up, w_down, learn_rate, window_len[head_order])
    return restore(head_order, mixed)


def solution(mesh):
    both = P(("seq", "head"), None)
    placed = (both, both, both, both, P("seq"), P(), P(), P()) + (P("head", None, None),) * 3
    return jax.shard_map(per_device, mesh=mesh, in_specs=placed, out_specs=both, check_vma=False)
```

time: 706 us -> 207 us (0.29)
  the two profiles are of different devices: /device:TPU:4 before, /device:TPU:12 now
where the time goes in v2:
time: 207 us
  Pallas kernels  203 us (98%)
  other arithmetic  2.81 us (1%)
    pallas_call x1, Pallas kernels, layer(): pl.pallas_call(layer_kernel, in_specs=[ANY] * 5 + [smem] * 2, out_specs=A...  191 us
    pallas_call x1, Pallas kernels, reorder(): pl.pallas_call(reorder_kernel, grid_spec=pltpu.PrefetchScalarGridSpec(num...  7.13 us
    pallas_call x1, Pallas kernels, restore(): pl.pallas_call(restore_kernel, grid_spec=pltpu.PrefetchScalarGridSpec(num...  4.24 us

profile of v2, /device:TPU:12, one launch (start us, length us, event | category | flops | bytes accessed | tf_op | source)
XLA Modules:
  0.0 206.7 jit_solution(2583786371413309170)
XLA Ops:
  0.0 0.0 copy-start
  0.0 0.7 compare_select_fusion
  0.7 0.8 and_select_fusion.1
  1.5 0.0 copy-done
  1.5 1.3 gather_fusion
  2.8 1.4 fusion.rate
  4.1 7.1 %reorder.1 = (bf16[8,272,640]{2,1,0:T(8,128)(2,1)}, bf16[8,128,640]{2,1,0:T(8,128)(2,1)}) custom-call(s32[40]{0:T(128)} %order.3, bf16[128,5120]{1,0:T(8,128)(2,1)} %q.1, bf16[128,5120]{1,0:T(8,128)(2,1)} %k.1, bf16[128,5120]{1,0:T(8,128)(2,1)} %v.1, bf16[8,16,128]{2,1,0:T(8,128)(2,1)} %fusion.rate), custom_call_target="tpu_custom_call" | custom-call | tf_op jit(solution)/shard_map/reorder/pallas_call | solution.py:62
  11.3 191.2 %layer.1.a = bf16[8,128,640]{2,1,0:T(8,128)(2,1)} custom-call(bf16[8,272,640]{2,1,0:T(8,128)(2,1)} %get-tuple-element.7.kvr, bf16[8,128,640]{2,1,0:T(8,128)(2,1)} %get-tuple-element.8.q, bf16[2,640,640]{2,1,0:T(8,128)(2,1)} %wg.1, bf16[2,640,640]{2,1,0:T(8,128)(2,1)} %wu.1, bf16[2,640,640]{2,1,0:T(8,128)(2,1)} %wd.1, f32[8]{0:T(128)} %rates.1, s32[40]{0:T(128)} %gather_fusion), custom_call_target="tpu_custom_call" | custom-call | tf_op jit(solution)/shard_map/layer/pallas_call | solution.py:489
  202.5 4.2 %restore.1 = bf16[128,5120]{1,0:T(8,128)(2,1)} custom-call(s32[40]{0:T(128)} %order.3, bf16[8,128,640]{2,1,0:T(8,128)(2,1)} %layer.1.a), custom_call_target="tpu_custom_call" | custom-call | tf_op jit(solution)/shard_map/restore/pallas_call | solution.py:510
  (3 shorter events, 0.0 us)
Async XLA Ops:
  0.0 1.5 copy-start

commit v3 on v2

--- a/solution.py
+++ b/solution.py
@@ -19,7 +19,8 @@
 F32 = jnp.float32
 BF16 = jnp.bfloat16
 
-SEND_ORDER = ((0, 1), (1, 0), (3, 0), (1, 1), (3, 1), (2, 0), (2, 1))
+SEND_ORDER = ((0, 1), (1, 0), (3, 0), (2, 1), (1, 1), (2, 0), (3, 1))
+WAVES = ((0, 1, 2, 4), (3, 5, 6))
 
 
 def coords():
@@ -100,8 +101,8 @@
 
 def layer_kernel(
     kvr, q, wg, wu, wd, rates, wins, out,
-    w2, w1, w0, qb, wb, kn, hid, tgt, bgu, grad, r0, h, r1, tot, part, r2, gsum, new, docs, kh, vh, ms, ls, accs, att, mixed,
-    s_l, s_kv, s_q, s_f, s_g, s_r, s_w, r_kv, r_q, r_w0, r_w1, r_w, s0, t0, s1, t1, s2, t2, s3, t3, s4, t4, s_o, r_o,
+    w2, w1, w0, qb, wb, kn, hid, tgt, bgu, grad, r0, h, r1, tot, part, r2, gsum, new, docs, kh, vh, ms, ls, accs, att, mixed, rb,
+    s_l, s_kv, s_q, s_f, s_g, s_r, s_w, r_kv, r_q, r_w0, r_w1, r_w, s0, t0, s1, t1, s2, t2, s3, t3, s4, t4, s_o, r_o, s_rb, r_rb,
 ):
     row, z, x, c = coords()
     half = lax.div(z, 2)
@@ -131,6 +132,18 @@
         signal(barrier, dev(row - 1, z, x, 0))
         signal(barrier, dev(row - 1, z, x, 1))
 
+    @pl.when(row == 7)
+    def _():
+        signal(barrier, dev(3, z, 1 - x, c))
+
+    @pl.when((row == 4) & (c == 0))
+    def _():
+        signal(barrier, dev(0, z, x, 1))
+        signal(barrier, dev(7, z, 1 - x, 0))
+        signal(barrier, dev(7, z, 1 - x, 1))
+
+    carrier = (row == 0) | (row == 7)
+
     @pl.when(own)
     def _():
         pltpu.make_async_copy(kvr.at[mine], w2.at[block], r_kv.at[block]).start()
@@ -146,7 +159,7 @@
     def _():
         w1[...] = jnp.zeros_like(w1)
 
-    pl.semaphore_wait(barrier, 19 + one(jnp.logical_not(last)))
+    pl.semaphore_wait(barrier, 19 + one(jnp.logical_not(last)) + one(row == 3) + one((row == 0) & (c == 1)) + one(last))
 
     def target(dz, dx):
         zt, xt = lax.rem(z + dz, 4), lax.rem(x + dx, 2)
@@ -156,45 +169,56 @@
     def _():
         rcopy(kvr.at[mine], w2.at[block], s_kv.at[7], r_kv.at[block], partner).start()
 
-    for n, (dz, dx) in enumerate(SEND_ORDER):
-        g, to = target(dz, dx)
-        rcopy(kvr.at[g], w2.at[block], s_kv.at[n], r_kv.at[block], to).start()
+    def wave(w):
+        for n in WAVES[w]:
+            g, to = target(*SEND_ORDER[n])
+            rcopy(kvr.at[g], w2.at[block], s_kv.at[n], r_kv.at[block], to).start()
+
+    wave(0)
 
     @pl.when(own)
     def _():
         for n, w in enumerate((wg, wu, wd)):
             rcopy(w.at[lax.rem(z, 2)], wb.at[n], s_w.at[n], r_w.at[n], partner).start()
 
-    for n, (dz, dx) in enumerate(SEND_ORDER):
-        g, to = target(dz, dx)
-        rcopy(q.at[g], qb.at[block], s_q.at[n], r_q.at[block], to).start()
-
-    @pl.when(jnp.logical_not(own))
-    def _():
-        rcopy(q.at[mine], qb.at[block], s_q.at[7], r_q.at[block], partner).start()
-
     for n in range(3):
         sem_wait_bytes(wb.at[n], r_w.at[n])
 
+    def nth(n, local, z_first, x=x):
+        p = lax.div(n, 2)
+        zs = lax.rem(z_first + jnp.where(local, lax.div(p, 2), lax.rem(lax.div(p + 1, 2), 2)), 2)
+        return zs * 4 + lax.rem(x + p, 2) * 2 + lax.rem(n, 2)
+
     near = jnp.where(own, lax.rem(z, 2), jnp.where(z == 0, 1, jnp.where(z == 3, 0, 1 - lax.rem(z, 2))))
 
-    def nth(n, z_first):
-        zs = lax.rem(z_first + lax.div(n, 4), 2)
-        xs = lax.rem(x + lax.rem(lax.div(n, 2), 2), 2)
-        return zs * 4 + xs * 2 + lax.rem(n, 2)
-
     def arrive(n, _):
-        b = nth(n, near)
+        @pl.when(n == 2 * one(own))
+        def _():
+            for k in WAVES[0]:
+                sem_wait_bytes(w2.at[k], s_kv.at[k])
+            wave(1)
+
+        b = nth(n, own, near)
         sem_wait_bytes(w2.at[b], r_kv.at[b])
         kv = w2.at[b, pl.ds(0, 2 * TB)]
 
-        @pl.when(jnp.logical_not(last) & (c == 0))
+        direct = jnp.logical_not(last) & ((row != 3) | (n >= 6))
+
+        @pl.when(direct & (c == 0))
         def _():
             rcopy(kv, w0.at[b], s_f.at[b], r_w0.at[b], dev(row + 1, z, x, 0)).start()
 
-        @pl.when(jnp.logical_not(last) & (c == 1))
+        @pl.when(direct & (c == 1))
         def _():
             rcopy(kv, w1.at[b], s_f.at[b], r_w1.at[b], dev(row + 1, z, x, 0)).start()
+
+        @pl.when((row == 3) & (n < 3))
+        def _():
+            rcopy(kv, rb.at[n], s_f.at[b], r_rb.at[n], dev(0, z, x, c)).start()
+
+        @pl.when((row == 3) & (n >= 3) & (n < 6))
+        def _():
+            rcopy(kv, rb.at[n - 3], s_f.at[b], r_rb.at[n - 3], dev(7, z, 1 - x, c)).start()
 
         @pl.when(c == 0)
         def _():
@@ -221,6 +245,32 @@
 
     lax.fori_loop(0, 8, arrive, 0)
 
+    @pl.when(carrier)
+    def _():
+        for m in range(3):
+            far = row == 7
+            xs = jnp.where(far, 1 - x, x)
+            b = nth(m + 3 * one(far), own, near, xs)
+            sem_wait_bytes(rb.at[m], r_rb.at[m])
+
+            @pl.when(c == 0)
+            def _():
+                rcopy(rb.at[m], w0.at[b], s_rb.at[m], r_w0.at[b], dev(4, z, xs, 0)).start()
+
+            @pl.when(c == 1)
+            def _():
+                rcopy(rb.at[m], w1.at[b], s_rb.at[m], r_w1.at[b], dev(4, z, xs, 0)).start()
+
+    for k in WAVES[1]:
+        sem_wait_bytes(w2.at[k], s_kv.at[k])
+    for n, (dz, dx) in enumerate(SEND_ORDER):
+        g, to = target(dz, dx)
+        rcopy(q.at[g], qb.at[block], s_q.at[n], r_q.at[block], to).start()
+
+    @pl.when(jnp.logical_not(own))
+    def _():
+        rcopy(q.at[mine], qb.at[block], s_q.at[7], r_q.at[block], partner).start()
+
     def grad_rows(i, _):
         at = pl.ds(pl.multiple_of(i * HD, HD), HD)
         both = dot(kn[:, at], bgu[...], ((0,), (0,)))
@@ -271,7 +321,7 @@
     @pl.when((c == 0) & (row > 0))
     def _():
         def relay(n, _):
-            b = nth(n, jnp.where(half == 1, lax.rem(z, 2), 1 - z))
+            b = nth(n, half == 1, jnp.where(half == 1, lax.rem(z, 2), 1 - z))
             sem_wait_bytes(w1.at[b], r_w1.at[b])
             rcopy(w1.at[b], w0.at[b], s_r.at[b], r_w0.at[b], partner).start()
             return 0
@@ -382,7 +432,7 @@
         lax.fori_loop(0, GH, move, 0)
 
     def tile(n, _):
-        b = nth(7 - n, near)
+        b = nth(7 - n, own, near)
         qn = normed(qb[b])
         gate = dot(qn, new[0], ((1,), (0,)))
         up = dot(qn, new[1], ((1,), (0,)))
@@ -406,6 +456,11 @@
     for g in range(8):
         sem_wait_bytes(mixed.at[g], r_o.at[g])
 
+    @pl.when(carrier)
+    def _():
+        for m in range(3):
+            sem_wait_bytes(rb.at[m], s_rb.at[m])
+
     for b in range(8):
 
         @pl.when(jnp.logical_not(own & (block == b)))
@@ -413,7 +468,6 @@
             sem_wait_bytes(mixed.at[b], s_o.at[b])
 
     for n in range(7):
-        sem_wait_bytes(w2.at[n], s_kv.at[n])
         sem_wait_bytes(qb.at[n], s_q.at[n])
 
     @pl.when(jnp.logical_not(own))
@@ -482,9 +536,10 @@
         ((4, TQ, HD), F32),
         (half, F32),
         ((8, TB, FW), BF16),
+        ((3, 2 * TB, FW), BF16),
     ]
     d4, d8, d3 = dma((4,)), dma((8,)), dma((3,))
-    sems = [d3, d8, d8, d8, d8, d8, d3, d8, d8, d8, d8, d3, d4, d4, d4, d4, dma, dma, d4, d4, d4, d4, d8, d8]
+    sems = [d3, d8, d8, d8, d8, d8, d3, d8, d8, d8, d8, d3, d4, d4, d4, d4, dma, dma, d4, d4, d4, d4, d8, d8, d3, d3]
     smem = pl.BlockSpec(memory_space=pltpu.SMEM)
     return pl.pallas_call(
         layer_kernel,

time: 207 us -> 176 us (0.85)
  the two profiles are of different devices: /device:TPU:12 before, /device:TPU:22 now
where the time goes in v3:
time: 176 us; the launch traced here: 175 us
  Pallas kernels  171 us (97%)
  other arithmetic  2.81 us (2%)
    pallas_call x1, Pallas kernels, layer(): pl.pallas_call(layer_kernel, in_specs=[ANY] * 5 + [smem] * 2, out_specs=A...  160 us
    pallas_call x1, Pallas kernels, reorder(): pl.pallas_call(reorder_kernel, grid_spec=pltpu.PrefetchScalarGridSpec(num...  7.13 us
    pallas_call x1, Pallas kernels, restore(): pl.pallas_call(restore_kernel, grid_spec=pltpu.PrefetchScalarGridSpec(num...  4.24 us

profile of v3, /device:TPU:22, one launch (start us, length us, event | category | flops | bytes accessed | tf_op | source)
XLA Modules:
  0.0 175.3 jit_solution(3257109711698720152)
XLA Ops:
  0.0 0.0 copy-start
  0.0 0.7 compare_select_fusion
  0.7 0.8 and_select_fusion.1
  1.5 0.0 copy-done
  1.5 1.3 gather_fusion
  2.8 1.4 fusion.rate
  4.1 7.1 %reorder.1 = (bf16[8,272,640]{2,1,0:T(8,128)(2,1)}, bf16[8,128,640]{2,1,0:T(8,128)(2,1)}) custom-call(s32[40]{0:T(128)} %order.3, bf16[128,5120]{1,0:T(8,128)(2,1)} %q.1, bf16[128,5120]{1,0:T(8,128)(2,1)} %k.1, bf16[128,5120]{1,0:T(8,128)(2,1)} %v.1, bf16[8,16,128]{2,1,0:T(8,128)(2,1)} %fusion.rate), custom_call_target="tpu_custom_call" | custom-call | tf_op jit(solution)/shard_map/reorder/pallas_call | solution.py:63
  11.3 159.8 %layer.1.a = bf16[8,128,640]{2,1,0:T(8,128)(2,1)} custom-call(bf16[8,272,640]{2,1,0:T(8,128)(2,1)} %get-tuple-element.7.kvr, bf16[8,128,640]{2,1,0:T(8,128)(2,1)} %get-tuple-element.8.q, bf16[2,640,640]{2,1,0:T(8,128)(2,1)} %wg.1, bf16[2,640,640]{2,1,0:T(8,128)(2,1)} %wu.1, bf16[2,640,640]{2,1,0:T(8,128)(2,1)} %wd.1, f32[8]{0:T(128)} %rates.1, s32[40]{0:T(128)} %gather_fusion), custom_call_target="tpu_custom_call" | custom-call | tf_op jit(solution)/shard_map/layer/pallas_call | solution.py:544
  171.1 4.2 %restore.1 = bf16[128,5120]{1,0:T(8,128)(2,1)} custom-call(s32[40]{0:T(128)} %order.3, bf16[8,128,640]{2,1,0:T(8,128)(2,1)} %layer.1.a), custom_call_target="tpu_custom_call" | custom-call | tf_op jit(solution)/shard_map/restore/pallas_call | solution.py:565
  (3 shorter events, 0.0 us)
Async XLA Ops:
  0.0 1.5 copy-start

commit v4 on v3

--- a/solution.py
+++ b/solution.py
@@ -46,38 +46,6 @@
     )
 
 
-def reorder_kernel(order, q, k, v, rate, kvr, qo):
-    g = pl.program_id(0)
-    for j in range(GH):
-        at = pl.ds(pl.multiple_of(order[g * GH + j] * HD, HD), HD)
-        to = slice(j * HD, (j + 1) * HD)
-        kvr[0, 0:TB, to] = k[:, at]
-        kvr[0, TB : 2 * TB, to] = v[:, at]
-        qo[0, :, to] = q[:, at]
-    kvr[0, 2 * TB :, 0:HD] = rate[0]
-    kvr[0, 2 * TB :, HD:] = jnp.zeros((KVR - 2 * TB, FW - HD), BF16)
-
-
-def reorder(head_order, q, k, v, rate):
-    whole = pl.BlockSpec((TB, 40 * HD), lambda g, o: (0, 0))
-    return pl.pallas_call(
-        reorder_kernel,
-        grid_spec=pltpu.PrefetchScalarGridSpec(
-            num_scalar_prefetch=1,
-            grid=(8,),
-            in_specs=[whole, whole, whole, pl.BlockSpec((1, 16, HD), lambda g, o: (g, 0, 0))],
-            out_specs=[
-                pl.BlockSpec((1, KVR, FW), lambda g, o: (g, 0, 0)),
-                pl.BlockSpec((1, TB, FW), lambda g, o: (g, 0, 0)),
-            ],
-        ),
-        out_shape=[
-            jax.ShapeDtypeStruct((8, KVR, FW), BF16),
-            jax.ShapeDtypeStruct((8, TB, FW), BF16),
-        ],
-        name="reorder",
-    )(head_order, q, k, v, rate)
-
 SCALE = HD**-0.5 * 1.4426950408889634
 TQ = 256
 TK = 512
@@ -100,8 +68,8 @@
 
 
 def layer_kernel(
-    kvr, q, wg, wu, wd, rates, wins, out,
-    w2, w1, w0, qb, wb, kn, hid, tgt, bgu, grad, r0, h, r1, tot, part, r2, gsum, new, docs, kh, vh, ms, ls, accs, att, mixed, rb,
+    qi, ki, vi, wg, wu, wd, extra, order_of, rates, window, out,
+    qin, kin, vin, kvr, q, w2, w1, w0, qb, wb, kn, hid, tgt, bgu, grad, r0, h, r1, tot, part, r2, gsum, new, docs, kh, vh, ms, ls, accs, att, mixed, rb,
     s_l, s_kv, s_q, s_f, s_g, s_r, s_w, r_kv, r_q, r_w0, r_w1, r_w, s0, t0, s1, t1, s2, t2, s3, t3, s4, t4, s_o, r_o, s_rb, r_rb,
 ):
     row, z, x, c = coords()
@@ -117,6 +85,15 @@
     last = row == ROWS - 1
     one = lambda p: p.astype(jnp.int32)
 
+    for n, (a, b) in enumerate(((ki, kin), (vi, vin), (qi, qin))):
+
+        def fetch(i, _):
+            at = pl.ds(pl.multiple_of(i * HD, HD), HD)
+            pltpu.make_async_copy(a.at[:, at], b.at[i], s_l.at[n]).start()
+            return 0
+
+        lax.fori_loop(0, 8 * GH, fetch, 0)
+
     barrier = pltpu.get_barrier_semaphore()
     for dz in range(4):
         for dx in range(2):
@@ -144,10 +121,27 @@
 
     carrier = (row == 0) | (row == 7)
 
+    def stage_kv(g, _):
+        kvr[g, 2 * TB : KVR, :] = jnp.zeros((KVR - 2 * TB, FW), BF16)
+        kvr[g, 2 * TB : KVR, 0:HD] = extra[g]
+        for j in range(GH):
+            to = slice(j * HD, (j + 1) * HD)
+            kvr[g, 0:TB, to] = kin[order_of[g * GH + j]]
+            kvr[g, TB : 2 * TB, to] = vin[order_of[g * GH + j]]
+        return 0
+
+    def stage_q(g, _):
+        for j in range(GH):
+            q[g, :, j * HD : (j + 1) * HD] = qin[order_of[g * GH + j]]
+        return 0
+
+    sem_wait_bytes(kin, s_l.at[0])
+    sem_wait_bytes(vin, s_l.at[1])
+    lax.fori_loop(0, 8, stage_kv, 0)
+
     @pl.when(own)
     def _():
         pltpu.make_async_copy(kvr.at[mine], w2.at[block], r_kv.at[block]).start()
-        pltpu.make_async_copy(q.at[mine], qb.at[block], r_q.at[block]).start()
         for n, w in enumerate((wg, wu, wd)):
             pltpu.make_async_copy(w.at[lax.rem(z, 2)], wb.at[n], r_w.at[n]).start()
 
@@ -180,6 +174,13 @@
     def _():
         for n, w in enumerate((wg, wu, wd)):
             rcopy(w.at[lax.rem(z, 2)], wb.at[n], s_w.at[n], r_w.at[n], partner).start()
+
+    sem_wait_bytes(qin, s_l.at[2])
+    lax.fori_loop(0, 8, stage_q, 0)
+
+    @pl.when(own)
+    def _():
+        pltpu.make_async_copy(q.at[mine], qb.at[block], r_q.at[block]).start()
 
     for n in range(3):
         sem_wait_bytes(wb.at[n], r_w.at[n])
@@ -263,14 +264,6 @@
 
     for k in WAVES[1]:
         sem_wait_bytes(w2.at[k], s_kv.at[k])
-    for n, (dz, dx) in enumerate(SEND_ORDER):
-        g, to = target(dz, dx)
-        rcopy(q.at[g], qb.at[block], s_q.at[n], r_q.at[block], to).start()
-
-    @pl.when(jnp.logical_not(own))
-    def _():
-        rcopy(q.at[mine], qb.at[block], s_q.at[7], r_q.at[block], partner).start()
-
     def grad_rows(i, _):
         at = pl.ds(pl.multiple_of(i * HD, HD), HD)
         both = dot(kn[:, at], bgu[...], ((0,), (0,)))
@@ -294,6 +287,14 @@
         else:
             tot[...] = total
 
+    for n, (dz, dx) in enumerate(SEND_ORDER):
+        g, to = target(dz, dx)
+        rcopy(q.at[g], qb.at[block], s_q.at[n], r_q.at[block], to).start()
+
+    @pl.when(jnp.logical_not(own))
+    def _():
+        rcopy(q.at[mine], qb.at[block], s_q.at[7], r_q.at[block], partner).start()
+
     def reduce_y():
         for k in (1, 3, 2):
             sem_wait_bytes(r1.at[k], t1.at[k])
@@ -318,6 +319,8 @@
         for k in range(4):
             sem_wait_bytes(r2, t4.at[k])
 
+    reduce_y()
+
     @pl.when((c == 0) & (row > 0))
     def _():
         def relay(n, _):
@@ -347,7 +350,7 @@
 
     def head(hh, _):
         at = pl.ds(pl.multiple_of(hh * HD, HD), HD)
-        win = wins[mine * GH + hh].astype(F32)
+        win = window[order_of[mine * GH + hh]].astype(F32)
         for n, w in enumerate((w0, w1, w2)):
             for b in range(8):
                 rows = slice(n * 1024 + b * TB, n * 1024 + (b + 1) * TB)
@@ -398,11 +401,8 @@
 
         @pl.when(hh == 1)
         def _():
-            reduce_y()
-
-        @pl.when(hh == 3)
-        def _():
             reduce_x()
+
 
         return 0
 
@@ -504,12 +504,17 @@
     sem_wait_bytes(r2, s2)
 
 
-def layer(kvr, q, wg, wu, wd, rates, wins):
+def layer(q, k, v, wg, wu, wd, extra, order, rates, window):
     dma = pltpu.SemaphoreType.DMA
     piece = (3, PART, FW)
     mats = (3, FW, FW)
     half = (8 * TB, FW)
     vmem = [
+        ((8 * GH, TB, HD), BF16),
+        ((8 * GH, TB, HD), BF16),
+        ((8 * GH, TB, HD), BF16),
+        ((8, KVR, FW), BF16),
+        ((8, TB, FW), BF16),
         ((8, KVR, FW), BF16),
         ((8, 2 * TB, FW), BF16),
         ((8, 2 * TB, FW), BF16),
@@ -543,7 +548,7 @@
     smem = pl.BlockSpec(memory_space=pltpu.SMEM)
     return pl.pallas_call(
         layer_kernel,
-        in_specs=[ANY] * 5 + [smem] * 2,
+        in_specs=[ANY] * 6 + [VM] + [smem] * 3,
         out_specs=ANY,
         out_shape=jax.ShapeDtypeStruct((8, TB, FW), BF16),
         scratch_shapes=[pltpu.VMEM(s, d) for s, d in vmem] + sems,
@@ -551,7 +556,7 @@
             collective_id=0, has_side_effects=True, vmem_limit_bytes=60 * 1024 * 1024
         ),
         name="layer",
-    )(kvr, q, wg, wu, wd, rates, wins)
+    )(q, k, v, wg, wu, wd, extra, order, rates, window)
 
 
 def restore_kernel(order, a, o):
@@ -580,8 +585,7 @@
     line = lax.broadcasted_iota(jnp.int32, (8, 16, TB), 1)
     digits = jnp.where(line == 1, (doc // TB)[None, None, :], (doc % TB)[None, None, :]).astype(BF16)
     extra = jnp.where(line == 0, step_rate.T[:, None, :], digits)
-    kvr, q = reorder(head_order, queries, keys, values, extra)
-    mixed = layer(kvr, q, w_gate, w_up, w_down, learn_rate, window_len[head_order])
+    mixed = layer(queries, keys, values, w_gate, w_up, w_down, extra, head_order, learn_rate, window_len)
     return restore(head_order, mixed)
 
 

time: 176 us -> 163 us (0.926)
  the two profiles are of different devices: /device:TPU:22 before, /device:TPU:4 now
where the time goes in v4:
time: 163 us
  Pallas kernels  161 us (99%)
  other arithmetic  2.15 us (1%)
    pallas_call x1, Pallas kernels, layer(): pl.pallas_call(layer_kernel, in_specs=[ANY] * 6 + [VM] + [smem] * 3, out_...  156 us
    pallas_call x1, Pallas kernels, restore(): pl.pallas_call(restore_kernel, grid_spec=pltpu.PrefetchScalarGridSpec(num...  4.24 us

profile of v4, /device:TPU:4, one launch (start us, length us, event | category | flops | bytes accessed | tf_op | source)
XLA Modules:
  0.0 162.7 jit_solution(10924856466389968062)
XLA Ops:
  0.0 0.8 and_select_fusion.1
  0.8 1.4 fusion.extra
  2.2 156.3 %layer.1.a = bf16[8,128,640]{2,1,0:T(8,128)(2,1)} custom-call(bf16[128,5120]{1,0:T(8,128)(2,1)} %qi.1, bf16[128,5120]{1,0:T(8,128)(2,1)} %ki.1, bf16[128,5120]{1,0:T(8,128)(2,1)} %vi.1, bf16[2,640,640]{2,1,0:T(8,128)(2,1)} %wg.1, bf16[2,640,640]{2,1,0:T(8,128)(2,1)} %wu.1, bf16[2,640,640]{2,1,0:T(8,128)(2,1)} %wd.1, bf16[8,16,128]{2,1,0:T(8,128)(2,1)} %fusion.extra, ...), custom_call_target="tpu_custom_call" | custom-call | tf_op jit(solution)/shard_map/layer/pallas_call | solution.py:549
  158.5 4.2 %restore.1 = bf16[128,5120]{1,0:T(8,128)(2,1)} custom-call(s32[40]{0:T(128)} %order.1, bf16[8,128,640]{2,1,0:T(8,128)(2,1)} %layer.1.a), custom_call_target="tpu_custom_call" | custom-call | tf_op jit(solution)/shard_map/restore/pallas_call | solution.py:570
  (2 shorter events, 0.0 us)

commit v5 on v4

--- a/solution.py
+++ b/solution.py
@@ -20,7 +20,7 @@
 BF16 = jnp.bfloat16
 
 SEND_ORDER = ((0, 1), (1, 0), (3, 0), (2, 1), (1, 1), (2, 0), (3, 1))
-WAVES = ((0, 1, 2, 4), (3, 5, 6))
+WAVES = ((0, 1, 2), (4, 6, 5, 3))
 
 
 def coords():
@@ -571,9 +571,9 @@
         restore_kernel,
         grid_spec=pltpu.PrefetchScalarGridSpec(
             num_scalar_prefetch=1,
-            grid=(4,),
-            in_specs=[pl.BlockSpec((8, TB // 4, FW), lambda i, o: (0, i, 0))],
-            out_specs=pl.BlockSpec((TB // 4, 40 * HD), lambda i, o: (i, 0)),
+            grid=(2,),
+            in_specs=[pl.BlockSpec((8, TB // 2, FW), lambda i, o: (0, i, 0))],
+            out_specs=pl.BlockSpec((TB // 2, 40 * HD), lambda i, o: (i, 0)),
         ),
         out_shape=jax.ShapeDtypeStruct((TB, 40 * HD), BF16),
         name="restore",

time: 163 us -> 159 us (0.975)
  Pallas kernels: 161 us -> 156 us
    pallas_call x1, Pallas kernels: 156 us -> 153 us  [layer(): pl.pallas_call(layer_kernel, in_specs=[ANY] * 6 + [VM] + [smem] * 3, out_...]
where the time goes in v5:
time: 159 us; the launch traced here: 158 us
  Pallas kernels  156 us (98%)
  other arithmetic  2.15 us (1%)
    pallas_call x1, Pallas kernels, layer(): pl.pallas_call(layer_kernel, in_specs=[ANY] * 6 + [VM] + [smem] * 3, out_...  153 us

profile of v5, /device:TPU:4, one launch (start us, length us, event | category | flops | bytes accessed | tf_op | source)
XLA Modules:
  0.0 158.0 jit_solution(6543187216238245048)
XLA Ops:
  0.0 0.8 and_select_fusion.1
  0.8 1.4 fusion.extra
  2.2 152.9 %layer.1.a = bf16[8,128,640]{2,1,0:T(8,128)(2,1)} custom-call(bf16[128,5120]{1,0:T(8,128)(2,1)} %qi.1, bf16[128,5120]{1,0:T(8,128)(2,1)} %ki.1, bf16[128,5120]{1,0:T(8,128)(2,1)} %vi.1, bf16[2,640,640]{2,1,0:T(8,128)(2,1)} %wg.1, bf16[2,640,640]{2,1,0:T(8,128)(2,1)} %wu.1, bf16[2,640,640]{2,1,0:T(8,128)(2,1)} %wd.1, bf16[8,16,128]{2,1,0:T(8,128)(2,1)} %fusion.extra, ...), custom_call_target="tpu_custom_call" | custom-call | tf_op jit(solution)/shard_map/layer/pallas_call | solution.py:549
  155.1 3.0 %restore.1 = bf16[128,5120]{1,0:T(8,128)(2,1)} custom-call(s32[40]{0:T(128)} %order.1, bf16[8,128,640]{2,1,0:T(8,128)(2,1)} %layer.1.a), custom_call_target="tpu_custom_call" | custom-call | tf_op jit(solution)/shard_map/restore/pallas_call | solution.py:570
  (2 shorter events, 0.0 us)

commit v6 on v5

--- a/solution.py
+++ b/solution.py
@@ -394,12 +394,12 @@
                 chunk(i, 1792 + TQ * i - TK * r, TK, False)
             return 0
 
-        lax.fori_loop(1, 4, back, 0)
+        lax.fori_loop(1, 4, back, 0, unroll=True)
         for i in range(4):
             chunk(i, TQ * i, TQ, False)
             att[i * TQ : (i + 1) * TQ, at] = accs[i] / jnp.sum(ls[i], axis=1, keepdims=True)
 
-        @pl.when(hh == 1)
+        @pl.when(hh == 0)
         def _():
             reduce_x()
 

time: 159 us -> 155 us (0.975)
  Pallas kernels: 156 us -> 153 us
    pallas_call x1, Pallas kernels: 153 us -> 150 us  [layer(): pl.pallas_call(layer_kernel, in_specs=[ANY] * 6 + [VM] + [smem] * 3, out_...]
where the time goes in v6:
time: 155 us
  Pallas kernels  153 us (99%)
  other arithmetic  2.15 us (1%)
    pallas_call x1, Pallas kernels, layer(): pl.pallas_call(layer_kernel, in_specs=[ANY] * 6 + [VM] + [smem] * 3, out_...  150 us

profile of v6, /device:TPU:4, one launch (start us, length us, event | category | flops | bytes accessed | tf_op | source)
XLA Modules:
  0.0 154.7 jit_solution(11309393652489918396)
XLA Ops:
  0.0 0.8 and_select_fusion.1
  0.8 1.4 fusion.extra
  2.2 149.6 %layer.1.a = bf16[8,128,640]{2,1,0:T(8,128)(2,1)} custom-call(bf16[128,5120]{1,0:T(8,128)(2,1)} %qi.1, bf16[128,5120]{1,0:T(8,128)(2,1)} %ki.1, bf16[128,5120]{1,0:T(8,128)(2,1)} %vi.1, bf16[2,640,640]{2,1,0:T(8,128)(2,1)} %wg.1, bf16[2,640,640]{2,1,0:T(8,128)(2,1)} %wu.1, bf16[2,640,640]{2,1,0:T(8,128)(2,1)} %wd.1, bf16[8,16,128]{2,1,0:T(8,128)(2,1)} %fusion.extra, ...), custom_call_target="tpu_custom_call" | custom-call | tf_op jit(solution)/shard_map/layer/pallas_call | solution.py:549
  151.7 3.0 %restore.1 = bf16[128,5120]{1,0:T(8,128)(2,1)} custom-call(s32[40]{0:T(128)} %order.1, bf16[8,128,640]{2,1,0:T(8,128)(2,1)} %layer.1.a), custom_call_target="tpu_custom_call" | custom-call | tf_op jit(solution)/shard_map/restore/pallas_call | solution.py:570
  (2 shorter events, 0.0 us)
